TPU v7x, 32 devices: a whole 2x2x4 slice. The times are simulated.
32 devices in a mesh: chan: 4 (over y, x), panel: 8 (over z, core).
Axes of the slice: x: 2, y: 2, z: 4, core: 2. Of those that a mesh axis runs over, the one named last changes fastest.
Arguments:
- voltages: bfloat16 [512, 536576], P(('chan', 'panel')), may hold values from -6 to 6
- prototype: float32 [4, 4096], replicated, may hold values from -0.046875 to 0.046875
- complex_gains: float32 [512, 48], P(('chan', 'panel')), may hold values from -4 to 4
- flagged: int32 [256], P(('chan', 'panel')), may hold values 0 or 1
- station_order: int32 [256], replicated, may hold values from 0 to 255, each once
Outputs:
- visibilities: bfloat16 [2, 24, 512, 512], P(None, 'chan', 'panel')
Inputs may be any that keep to these rules, and one draw needn't show every extreme that they name: `station_order`: each station appears once.
All inputs are finite; a program needn't handle non-finite values. No bound on the sum of `flagged` on one device may be relied on, other than what follows from the above.
Results may differ from a plain program's by a relative error of at most 0.0073.
Values may be sent and summed in bfloat16 or wider, within the bound.
No kernel may reach another device: no remote copies, remote signals or barrier semaphores. Data moves between devices by JAX's collectives and lax.ppermute only.
A program may use at most 128 MiB of HBM per device.

v0:
```python
import math

import jax
import jax.numpy as jnp
from jax import lax
from jax.sharding import PartitionSpec as P

BLOCKS = 2


def make_table(length, channels):
    sample = jnp.arange(length, dtype=jnp.int32)[:, None]
    column = length // 4 + jnp.arange(channels, dtype=jnp.int32)[None, :]
    phases = (sample * column % length).astype(jnp.float32) * (2.0 * math.pi / length)
    stacked = jnp.stack([jnp.cos(phases), -jnp.sin(phases)], axis=2)
    return stacked.reshape(length, 2 * channels).astype(jnp.bfloat16)


def windowed(shaped_volt, prototype, first_frame, count):
    accumulated = jnp.zeros((shaped_volt.shape[0], count, shaped_volt.shape[2]), jnp.float32)
    for tap_index in range(prototype.shape[0]):
        start = first_frame + tap_index
        accumulated = accumulated + prototype[tap_index][None, None, :] * shaped_volt[
            :, start : start + count, :
        ].astype(jnp.float32)
    return accumulated.astype(jnp.bfloat16)


def spectra_of(shaped_volt, prototype, dft_table, complex_gains, keeping, first_frame, count):
    frames_win = windowed(shaped_volt, prototype, first_frame, count)
    raw_spectra = jnp.einsum(
        "nk,ifn->kif", dft_table, frames_win, preferred_element_type=jnp.float32
    )
    channels = dft_table.shape[1] // 2
    local_inputs = shaped_volt.shape[0]
    shaped = raw_spectra.reshape(channels, 2, local_inputs, count)
    gain_parts = complex_gains.T.reshape(channels, 2, local_inputs)[:, :, :, None]
    real_part = gain_parts[:, 0] * shaped[:, 0] - gain_parts[:, 1] * shaped[:, 1]
    imag_part = gain_parts[:, 0] * shaped[:, 1] + gain_parts[:, 1] * shaped[:, 0]
    stacked = jnp.stack([real_part, imag_part], axis=2) * keeping[None, :, None, None]
    return stacked.reshape(channels, local_inputs, 2 * count).astype(jnp.bfloat16)


def local(voltages, prototype, complex_gains, flagged, station_order):
    local_inputs = voltages.shape[0]
    length = prototype.shape[1]
    tap_count = prototype.shape[0]
    channels = complex_gains.shape[1] // 2
    frame_total = voltages.shape[1] // length - tap_count + 1
    shaped_volt = voltages.reshape(local_inputs, frame_total + tap_count - 1, length)
    keeping = jnp.repeat(1.0 - flagged.astype(jnp.float32), 2)
    dft_table = make_table(length, channels)
    chan_size = lax.axis_size("chan")
    panel_size = lax.axis_size("panel")
    inputs_all = 2 * station_order.shape[0]
    panel_width = inputs_all // panel_size
    position = jnp.arange(inputs_all, dtype=jnp.int32)
    source = 2 * station_order[position // 2] + position % 2
    device_of = source // local_inputs
    within = source % local_inputs
    local_row = (
        device_of % panel_size * (chan_size * local_inputs)
        + device_of // panel_size * local_inputs
        + within
    )
    mine = lax.dynamic_slice_in_dim(local_row, lax.axis_index("panel") * panel_width, panel_width)
    block_len = frame_total // BLOCKS
    accumulated = None
    for block_index in range(BLOCKS):
        spectra = spectra_of(
            shaped_volt,
            prototype,
            dft_table,
            complex_gains,
            keeping,
            block_index * block_len,
            block_len,
        )
        turned = lax.all_to_all(spectra, "chan", split_axis=0, concat_axis=1, tiled=True)
        gathered = lax.all_gather(turned, "panel", axis=1, tiled=True)
        columns = jnp.take(gathered, local_row, axis=1)
        picked = jnp.take(gathered, mine, axis=1)
        count = picked.shape[2] // 2
        swapped = jnp.concatenate([picked[:, :, count:], -picked[:, :, :count]], axis=2)
        left = jnp.stack([picked, swapped], axis=1)
        product = jnp.einsum("cspt,cqt->scpq", left, columns, preferred_element_type=jnp.float32)
        accumulated = product if accumulated is None else accumulated + product
    return (accumulated * (1.0 / frame_total)).astype(jnp.bfloat16)


def solution(mesh):
    placed = (
        P(("chan", "panel"), None),
        P(),
        P(("chan", "panel"), None),
        P(("chan", "panel")),
        P(),
    )
    return jax.shard_map(
        local, mesh=mesh, in_specs=placed, out_specs=P(None, "chan", "panel", None), check_vma=False
    )
```

profile of v0, /device:TPU:0, one launch (start us, length us, event | category | flops | bytes accessed | tf_op | source)
XLA Modules:
  0.0 116.8 jit_solution(329079163011565465)
XLA Ops:
  0.0 1.1 fusion.44
  1.1 1.9 %cosine_convert_fusion = (bf16[4096,24,1]{0,1,2:T(8,128)(2,1)S(1)}, bf16[4096,24,1]{0,1,2:T(8,128)(2,1)S(1)}) fusion(s32[24]{0:T(128)S(1)} %iota_add_fusion), kind=kLoop, calls=%fused_computation.28 | loop fusion | flops 1671168 | bytes 393312 | tf_op jit(solution)/shard_map/convert
  3.0 0.4 copy.51
  3.4 0.1 convert_element_type.66
  3.5 0.3 dot_general.17
  3.8 21.9 %reshape.270 = bf16[16,131,4096]{2,1,0:T(8,128)(2,1)} reshape(bf16[16,536576]{1,0:T(8,128)(2,1)} %param.9) | data formatting | bytes 34340864 | tf_op jit(solution)/shard_map/reshape | solution.py:50
  25.8 16.5 %fusion.4 = f32[24,2,16,64]{3,0,2,1:T(8,128)S(1)} fusion(bf16[16,131,4096]{2,1,0:T(8,128)(2,1)} %reshape.270, f32[4096]{0:T(1024)S(1)} %bitcast.94, f32[4096]{0:T(1024)S(1)} %bitcast.96, f32[4096]{0:T(1024)S(1)} %bitcast.92, f32[4096]{0:T(1024)S(1)} %bitcast.90, bf16[24,2,4096,1]{2,1,0,3:T(2,128)(2,1)S(1)} %bitcast.81), kind=kOutput, calls=%fused_computation.10 | convolution fusion | flops 452984832 | bytes 34209792 | tf_op jit(solution)/shard_map/nk,ifn->kif/dot_general | solution.py:31
  42.3 16.8 %fusion.2 = f32[24,2,16,64]{3,0,2,1:T(8,128)S(1)} fusion(bf16[16,131,4096]{2,1,0:T(8,128)(2,1)} %reshape.270, f32[4096]{0:T(1024)S(1)} %bitcast.95, f32[4096]{0:T(1024)S(1)} %bitcast.97, f32[4096]{0:T(1024)S(1)} %bitcast.93, f32[4096]{0:T(1024)S(1)} %bitcast.91, bf16[24,2,4096,1]{2,1,0,3:T(2,128)(2,1)S(1)} %bitcast.82), kind=kOutput, calls=%fused_computation.9 | convolution fusion | flops 452984832 | bytes 34209792 | tf_op jit(solution)/shard_map/nk,ifn->kif/dot_general | solution.py:31
  59.4 0.2 multiply_subtract_fusion
  59.6 0.3 copy.54
  59.9 0.2 stack.40
  60.2 0.3 copy.62
  60.5 0.2 stack.45
  60.9 0.8 multiply_convert_fusion.1
  61.7 5.2 %all-to-all-start = ((bf16[24,16,128]{2,1,0:T(8,128)(2,1)}), bf16[24,16,128]{2,1,0:T(8,128)(2,1)S(1)}, u32[]{:S(2)}, u32[]{:S(2)}) async-start(bf16[24,16,128]{2,1,0:T(8,128)(2,1)} %get-tuple-element.36), calls=%async_computation | async-start | bytes 196608 | tf_op jit(solution)/shard_map/all_to_all | solution.py:79
  66.9 3.5 %gather_fusion = s32[512]{0:T(512)S(1)} fusion(s32[256]{0:T(256)S(1)} %copy-done, s32[1024]{0:T(1024)S(1)} %pad_clamp_fusion.2), kind=kCustom, calls=%fused_computation.4 | custom fusion | bytes 6144 | tf_op jit(solution)/shard_map/gather | solution.py:58
  70.6 1.2 %all-to-all-done = bf16[24,16,128]{2,1,0:T(8,128)(2,1)S(1)} async-done(((bf16[24,16,128]{2,1,0:T(8,128)(2,1)}), bf16[24,16,128]{2,1,0:T(8,128)(2,1)S(1)}, u32[]{:S(2)}, u32[]{:S(2)}) %all-to-all-start) | async-done | bytes 98336 | tf_op jit(solution)/shard_map/all_to_all | solution.py:79
  71.8 3.3 %all-to-all-start.1 = ((bf16[24,16,128]{2,1,0:T(8,128)(2,1)}), bf16[24,16,128]{2,1,0:T(8,128)(2,1)S(1)}, u32[]{:S(2)}, u32[]{:S(2)}) async-start(bf16[24,16,128]{2,1,0:T(8,128)(2,1)} %get-tuple-element.35), calls=%async_computation.1 | async-start | bytes 196608 | tf_op jit(solution)/shard_map/all_to_all | solution.py:79
  75.1 16.1 %all_gather.6 = bf16[6,512,128]{2,1,0:T(8,128)(2,1)S(1)} all-gather(bf16[6,64,128]{2,1,0:T(8,128)(2,1)S(1)} %bitcast.85), channel_id=1, replica_groups=mesh['chan'=4,'panel'=8] {'panel'}, dimensions={1}, use_global_device_ids=true | all-gather | bytes 884736 | tf_op jit(solution)/shard_map/all_gather | solution.py:80
  91.2 0.5 copy.56
  91.8 15.5 %all_gather.7 = bf16[6,512,128]{2,1,0:T(8,128)(2,1)S(1)} all-gather(bf16[6,64,128]{2,1,0:T(8,128)(2,1)S(1)} %bitcast.86), channel_id=1, replica_groups=mesh['chan'=4,'panel'=8] {'panel'}, dimensions={1}, use_global_device_ids=true | all-gather | bytes 884736 | tf_op jit(solution)/shard_map/all_gather | solution.py:80
  107.3 0.5 copy.64
  107.8 0.6 gather_fusion.2
  108.5 0.6 gather_fusion.4
  109.1 1.8 %gather_fusion.1 = bf16[512,6,128]{2,1,0:T(8,128)(2,1)S(1)} fusion(bf16[6,512,128]{2,0,1:T(8,128)(2,1)S(1)} %copy.56, s32[1024]{0:T(1024)S(1)} %pad_clamp_fusion.1), kind=kCustom, calls=%fused_computation.clone | custom fusion | bytes 1574912 | tf_op jit(solution)/shard_map/jit(_take)/gather | solution.py:81
  110.9 1.8 %gather_fusion.3 = bf16[512,6,128]{2,1,0:T(8,128)(2,1)S(1)} fusion(bf16[6,512,128]{2,0,1:T(8,128)(2,1)S(1)} %copy.64, s32[1024]{0:T(1024)S(1)} %pad_clamp_fusion.1), kind=kCustom, calls=%fused_computation.2.clone | custom fusion | bytes 1574912 | tf_op jit(solution)/shard_map/jit(_take)/gather | solution.py:81
  112.7 0.1 fusion.26
  113.1 0.1 maximum_bitcast_fusion
  113.2 1.8 %select_bitcast_fusion = (bf16[6,512,128,1]{2,0,1,3:T(8,128)(2,1)S(1)}, bf16[6,512,128,1]{2,0,1,3:T(8,128)(2,1)S(1)}) fusion(bf16[512,6,128]{2,1,0:T(8,128)(2,1)S(1)} %gather_fusion.3, pred[512]{0:T(512)(128)(4,1)S(1)} %get-tuple-element.9, bf16[512,6,128]{2,1,0:T(8,128)(2,1)S(1)} %gather_fusion.1), kind=kLoop, calls=%fused_computation.13 | loop fusion | flops 786432 | bytes 3146240 | tf_op jit(solution)/shard_map/jit(_take)/select_n | solution.py:81
  115.0 0.4 fusion.8
  115.4 0.4 fusion.6
  115.8 0.9 copy.69
  (29 shorter events, 1.0 us)
Async XLA Ops:
  0.0 66.9 %copy-start = (s32[256]{0:T(256)S(1)}, s32[256]{0:T(256)}, u32[]{:S(2)}) copy-start(s32[256]{0:T(256)} %param.13) | copy-start | bytes 3076
  42.3 16.8 %copy-start.1 = (f32[16,48]{1,0:T(8,128)S(1)}, f32[16,48]{1,0:T(8,128)}, u32[]{:S(2)}) copy-start(f32[16,48]{1,0:T(8,128)} %param.11) | copy-start | bytes 9220
  42.3 18.4 %copy-start.2 = (s32[8]{0:T(128)S(1)}, s32[8]{0:T(128)}, u32[]{:S(2)}) copy-start(s32[8]{0:T(128)} %param.12) | copy-start | bytes 100
  61.7 10.1 %all-to-all-start = ((bf16[24,16,128]{2,1,0:T(8,128)(2,1)}), bf16[24,16,128]{2,1,0:T(8,128)(2,1)S(1)}, u32[]{:S(2)}, u32[]{:S(2)}) async-start(bf16[24,16,128]{2,1,0:T(8,128)(2,1)} %get-tuple-element.36), calls=%async_computation | async-start | bytes 196608 | tf_op jit(solution)/shard_map/all_to_all | solution.py:79
  71.8 20.0 %all-to-all-start.1 = ((bf16[24,16,128]{2,1,0:T(8,128)(2,1)}), bf16[24,16,128]{2,1,0:T(8,128)(2,1)S(1)}, u32[]{:S(2)}, u32[]{:S(2)}) async-start(bf16[24,16,128]{2,1,0:T(8,128)(2,1)} %get-tuple-element.35), calls=%async_computation.1 | async-start | bytes 196608 | tf_op jit(solution)/shard_map/all_to_all | solution.py:79
where the time goes:
time: 117 us
  local copies, waits for them, and re-layouts  35.7 us (31%)
  matrix products  34.1 us (29%)
  blocking collectives  31.6 us (27%)
  starting transfers between devices  8.5 us (7%)
  other arithmetic  5.37 us (5%)
  waiting for transfers between devices  1.22 us (1%)
    dot_general x2, matrix products, spectra_of(): jnp.einsum('nk,ifn->kif', dft_table, frames_win, preferred_element_type=j...  33.3 us
    all_gather x2, blocking collectives, local(): gathered = lax.all_gather(turned, 'panel', axis=1, tiled=True)  31.6 us
    reshape x1, local copies, waits for them, and re-layouts, local(): voltages.reshape(local_inputs, frame_total + tap_count - 1, length)  21.9 us
    all_to_all x2, starting transfers between devices, local(): lax.all_to_all(spectra, 'chan', split_axis=0, concat_axis=1, tiled=True)  8.5 us
    gather x2, local copies, waits for them, and re-layouts, local(): columns = jnp.take(gathered, local_row, axis=1)  3.6 us
    gather x1, local copies, waits for them, and re-layouts, local(): source = 2 * station_order[position // 2] + position % 2  3.52 us
  transfers between devices with their start and end apart: 2, of which 1 were waited for; matrix products, arithmetic and copies ran while one was open for 4% of the time, Pallas kernels for 0%

commit v1 on v0

v1 whole, which is shorter than its diff:
```python
import functools
import math

import jax
import jax.numpy as jnp
import numpy as np
from jax import lax
from jax.experimental import pallas as pl
from jax.experimental.pallas import tpu as pltpu
from jax.sharding import PartitionSpec as P

GROUP = 33
DEPTH = 256
VMEM = pl.BlockSpec(memory_space=pltpu.VMEM)
SMEM = pl.BlockSpec(memory_space=pltpu.SMEM)


def table_rows(length, channels, rows):
    sample = np.arange(length, dtype=np.int64)[None, :]
    column = length // 4 + np.arange(channels, dtype=np.int64)[:, None]
    phases = (sample * column % length) * (2.0 * math.pi / length)
    table = np.zeros((rows, length), np.float32)
    table[:channels] = np.cos(phases)
    table[channels : 2 * channels] = -np.sin(phases)
    return jnp.asarray(table, jnp.bfloat16)


def partner(index, step, size):
    return index ^ step if size & (size - 1) == 0 else (index + step) % size


def slot_of(index, source, size):
    return index ^ source if size & (size - 1) == 0 else (index - source) % size


def channelize(
    me_ref, volt_ref, proto_ref, table_ref, gains_ref, flag_ref, *refs, groups, frames, stride
):
    outs = refs[:groups]
    buf, sems, weights, sums, stage, spectra = refs[groups:]
    inputs = volt_ref.shape[0]
    taps, length = proto_ref.shape
    used = gains_ref.shape[0]
    channels = used // 2
    need = frames + taps - 1
    steps = -(-need // GROUP)

    def fetch(step):
        part = pl.ds(step * GROUP * length, min(GROUP, need - step * GROUP) * length)
        return pltpu.make_async_copy(volt_ref.at[:, part], buf.at[:, part], sems.at[step])

    for step in range(steps):
        fetch(step).start()
    table = table_ref[...].astype(jnp.float32)
    for tap in range(taps):
        weights[tap * stride : (tap + 1) * stride, :] = (
            table * proto_ref[tap : tap + 1, :]
        ).astype(jnp.bfloat16)
    for step in range(steps):
        fetch(step).wait()
        count = min(GROUP, need - step * GROUP)
        total = None
        for low in range(0, length, DEPTH):
            rows = [
                buf[:, (step * GROUP + f) * length + low : (step * GROUP + f) * length + low + DEPTH]
                for f in range(count)
            ]
            part = lax.dot_general(
                jnp.concatenate(rows, axis=0),
                weights[:, low : low + DEPTH],
                (((1,), (1,)), ((), ())),
                preferred_element_type=jnp.float32,
            )
            total = part if total is None else total + part
        sums[step * GROUP : step * GROUP + count] = total.reshape(count, inputs, taps * stride)
    for first in range(0, frames, 16):
        count = min(16, frames - first)
        raw = None
        for tap in range(taps):
            piece = sums[first + tap : first + tap + count, :, tap * stride : tap * stride + used]
            raw = piece if raw is None else raw + piece
        stage[first * inputs : (first + count) * inputs, 0:used] = raw.reshape(count * inputs, used)
    for i in range(inputs):
        raw = stage[pl.ds(i, frames, stride=inputs), :].T[0:used, :]
        real, imag = raw[0:channels], raw[channels:used]
        gain_real = gains_ref[0:channels, i : i + 1]
        gain_imag = gains_ref[channels:used, i : i + 1]
        keep = 1.0 - flag_ref[i // 2].astype(jnp.float32)
        spectra[:, i, 0:frames] = ((gain_real * real - gain_imag * imag) * keep).astype(jnp.bfloat16)
        spectra[:, i, frames:] = ((gain_real * imag + gain_imag * real) * keep).astype(jnp.bfloat16)
    each = channels // groups
    for step in range(groups):
        outs[step][...] = spectra[pl.ds(partner(me_ref[0], step, groups) * each, each)]


def correlate(row_ref, mine_ref, *refs, frames):
    pieces, out_ref, select = refs[:-2], refs[-2], refs[-1]
    blocks, each, local = pieces[0].shape[:3]
    inputs = row_ref.shape[1]
    width = mine_ref.shape[0]
    select[...] = jnp.where(
        lax.broadcasted_iota(jnp.int32, (inputs, inputs), 0) == row_ref[...], 1.0, 0.0
    ).astype(jnp.bfloat16)
    pick = jnp.where(
        lax.broadcasted_iota(jnp.int32, (width, inputs), 1) == mine_ref[...], 1.0, 0.0
    ).astype(jnp.bfloat16)
    for j in range(each):
        columns = jnp.concatenate(
            [piece[b, j] for piece in pieces for b in range(blocks)], axis=0
        )
        picked = jnp.dot(pick, columns, preferred_element_type=jnp.float32).astype(jnp.bfloat16)
        swapped = jnp.concatenate([picked[:, frames:], -picked[:, :frames]], axis=1)
        left = jnp.concatenate([picked, swapped], axis=0)
        product = lax.dot_general(
            left, columns, (((1,), (1,)), ((), ())), preferred_element_type=jnp.float32
        )
        rounded = (product * (1.0 / frames)).astype(jnp.bfloat16)
        ordered = jnp.dot(rounded, select[...], preferred_element_type=jnp.float32)
        ordered = ordered.astype(jnp.bfloat16)
        out_ref[0, j] = ordered[:width]
        out_ref[1, j] = ordered[width:]


def local(voltages, prototype, complex_gains, flagged, station_order):
    inputs = voltages.shape[0]
    taps, length = prototype.shape
    used = complex_gains.shape[1]
    channels = used // 2
    frames = voltages.shape[1] // length - taps + 1
    chan_size = lax.axis_size("chan")
    panel_size = lax.axis_size("panel")
    chan_me = lax.axis_index("chan")
    panel_me = lax.axis_index("panel")
    each = channels // chan_size
    stride = 64 if used <= 64 else -(-used // 128) * 128
    need = frames + taps - 1
    steps = -(-need // GROUP)

    gains = complex_gains.reshape(inputs, channels, 2).transpose(2, 1, 0).reshape(used, inputs)
    spectra = pl.pallas_call(
        functools.partial(channelize, groups=chan_size, frames=frames, stride=stride),
        out_shape=[jax.ShapeDtypeStruct((each, inputs, 2 * frames), jnp.bfloat16)] * chan_size,
        in_specs=[SMEM, pl.BlockSpec(memory_space=pl.ANY), VMEM, VMEM, VMEM, SMEM],
        out_specs=[VMEM] * chan_size,
        scratch_shapes=[
            pltpu.VMEM((inputs, need * length), jnp.bfloat16),
            pltpu.SemaphoreType.DMA((steps,)),
            pltpu.VMEM((taps * stride, length), jnp.bfloat16),
            pltpu.VMEM((need, inputs, taps * stride), jnp.float32),
            pltpu.VMEM((frames * inputs, -(-used // 128) * 128), jnp.float32),
            pltpu.VMEM((channels, inputs, 2 * frames), jnp.bfloat16),
        ],
        compiler_params=pltpu.CompilerParams(vmem_limit_bytes=56 * 1024 * 1024),
        name="channelize",
    )(
        chan_me[None].astype(jnp.int32),
        voltages,
        prototype,
        table_rows(length, channels, stride),
        gains,
        flagged,
    )

    turned = [spectra[0]]
    for step in range(1, chan_size):
        pairs = [(i, partner(i, step, chan_size)) for i in range(chan_size)]
        turned.append(lax.ppermute(spectra[step], "chan", pairs))
    turned = jnp.stack(turned)

    cores = 2 if panel_size % 2 == 0 else 1
    chips = panel_size // cores
    pieces = [turned]
    for step in range(1, chips):
        pairs = [
            (i * cores + k, partner(i, step, chips) * cores + k)
            for i in range(chips)
            for k in range(cores)
        ]
        pieces.append(lax.ppermute(turned, "panel", pairs))
    if cores == 2:
        swap = [(i, i ^ 1) for i in range(panel_size)]
        pieces += [lax.ppermute(piece, "panel", swap) for piece in pieces]

    inputs_all = 2 * station_order.shape[0]
    width = inputs_all // panel_size
    source = (2 * station_order[:, None] + jnp.arange(2, dtype=jnp.int32)[None, :]).reshape(-1)
    device = source // inputs
    chan_from, panel_from = device // panel_size, device % panel_size
    piece = slot_of(panel_me % cores, panel_from % cores, cores) * chips + slot_of(
        panel_me // cores, panel_from // cores, chips
    )
    row = (
        piece * (chan_size * inputs)
        + slot_of(chan_me, chan_from, chan_size) * inputs
        + source % inputs
    )
    mine = lax.dynamic_slice_in_dim(row, panel_me * width, width)

    return pl.pallas_call(
        functools.partial(correlate, frames=frames),
        out_shape=jax.ShapeDtypeStruct((2, each, width, inputs_all), jnp.bfloat16),
        in_specs=[VMEM] * (2 + len(pieces)),
        out_specs=VMEM,
        scratch_shapes=[pltpu.VMEM((inputs_all, inputs_all), jnp.bfloat16)],
        compiler_params=pltpu.CompilerParams(vmem_limit_bytes=56 * 1024 * 1024),
        name="correlate",
    )(row[None, :], mine[:, None], *pieces)


def solution(mesh):
    placed = (
        P(("chan", "panel"), None),
        P(),
        P(("chan", "panel"), None),
        P(("chan", "panel")),
        P(),
    )
    return jax.shard_map(
        local, mesh=mesh, in_specs=placed, out_specs=P(None, "chan", "panel", None), check_vma=False
    )
```

time: 117 us -> 52.9 us (0.45)
  matrix products: 34.1 us -> 0 us
  local copies, waits for them, and re-layouts: 35.7 us -> 3.51 us
  blocking collectives: 31.6 us -> 0 us
  Pallas kernels: 0 us -> 19.2 us
  waiting for transfers between devices: 1.22 us -> 18.7 us
  other arithmetic: 5.37 us -> 1.59 us
    dot_general x4 -> x0, matrix products: 34.1 us -> none  [the longest x2 33.3 us: spectra_of(): jnp.einsum('nk,ifn->kif', dft_table, frames_win, preferred_element_type=j...]
    all_gather x2 -> x0, blocking collectives: 31.6 us -> none  [local(): gathered = lax.all_gather(turned, 'panel', axis=1, tiled=True)]
    reshape x1 -> x0, local copies, waits for them, and re-layouts: 21.9 us -> none  [local(): voltages.reshape(local_inputs, frame_total + tap_count - 1, length)]
    pallas_call x0 -> x2, Pallas kernels: none -> 19.2 us  [the longest x1 14.4 us: local(): pl.pallas_call(functools.partial(channelize, groups=chan_size, frames=fra...]
    ppermute x0 -> x10, waiting for transfers between devices: none -> 18.7 us  [the longest x3 13.2 us: local(): pieces.append(lax.ppermute(turned, 'panel', pairs))]
    ppermute x0 -> x10, starting transfers between devices: none -> 9.53 us  [the longest x3 4.57 us: local(): turned.append(lax.ppermute(spectra[step], 'chan', pairs))]
    all_to_all x2 -> x0, starting transfers between devices: 8.5 us -> none  [local(): lax.all_to_all(spectra, 'chan', split_axis=0, concat_axis=1, tiled=True)]
    gather x5 -> x0, local copies, waits for them, and re-layouts: 8.38 us -> none  [the longest x2 3.6 us: local(): columns = jnp.take(gathered, local_row, axis=1)]
  transfers between devices with their start and end apart: 2 -> 10, of which waited for: 1 -> 7; matrix products, arithmetic and copies ran while one was open for 4% -> 3% of each run, Pallas kernels for 0% -> 0%
where the time goes in v1:
time: 52.9 us; the launch traced here: 52.6 us
  Pallas kernels  19.2 us (36%)
  waiting for transfers between devices  18.7 us (35%)
  starting transfers between devices  9.53 us (18%)
  local copies, waits for them, and re-layouts  3.51 us (7%)
  other arithmetic  1.59 us (3%)
    pallas_call x1, Pallas kernels, local(): pl.pallas_call(functools.partial(channelize, groups=chan_size, frames=fra...  14.4 us
    ppermute x3, waiting for transfers between devices, local(): pieces.append(lax.ppermute(turned, 'panel', pairs))  13.2 us
    ppermute x3, waiting for transfers between devices, local(): turned.append(lax.ppermute(spectra[step], 'chan', pairs))  4.89 us
    pallas_call x1, Pallas kernels, local(): pl.pallas_call(functools.partial(correlate, frames=frames), out_shape=jax...  4.76 us
    ppermute x3, starting transfers between devices, local(): turned.append(lax.ppermute(spectra[step], 'chan', pairs))  4.57 us
    ppermute x3, starting transfers between devices, local(): pieces.append(lax.ppermute(turned, 'panel', pairs))  4.45 us
    unnamed x19, local copies, waits for them, and re-layouts  1.85 us
  transfers between devices with their start and end apart: 10, of which 7 were waited for; matrix products, arithmetic and copies ran while one was open for 3% of the time, Pallas kernels for 0%

profile of v1, /device:TPU:0, one launch (start us, length us, event | category | flops | bytes accessed | tf_op | source)
XLA Modules:
  0.0 52.6 jit_solution(16698267073708821496)
XLA Ops:
  0.0 0.8 %copy.9 = f32[16,48]{0,1:T(8,128)S(1)} copy(f32[16,48]{1,0:T(8,128)} %param.8) | data formatting | bytes 6144 | tf_op args[2]
  0.8 0.6 %copy.10 = f32[2,24,16]{2,1,0:T(8,128)} copy(f32[2,24,16]{2,0,1:T(2,128)S(1)} %bitcast.12) | data formatting | bytes 6144 | tf_op jit(solution)/shard_map/transpose | solution.py:139
  1.4 14.4 %channelize.1 = (bf16[6,16,256]{2,1,0:T(8,128)(2,1)}, bf16[6,16,256]{2,1,0:T(8,128)(2,1)}, bf16[6,16,256]{2,1,0:T(8,128)(2,1)}, bf16[6,16,256]{2,1,0:T(8,128)(2,1)}) custom-call(s32[1]{0:T(128)} %bitcast.1.me_ref, bf16[16,536576]{1,0:T(8,128)(2,1)} %volt_ref.1, f32[4,4096]{1,0:T(4,128)} %proto_ref.1, bf16[64,4096]{1,0:T(8,128)(2,1)} %constant.106.clone.table_ref, ...), custom_call_target="tpu_custom_call" | custom-call | tf_op jit(solution)/shard_map/channelize/pallas_call | solution.py:140
  15.9 3.0 %collective-permute-start = (bf16[6,16,256]{2,1,0:T(8,128)(2,1)}, bf16[6,16,256]{2,1,0:T(8,128)(2,1)S(1)}, u32[]{:S(2)}, u32[]{:S(2)}) collective-permute-start(bf16[6,16,256]{2,1,0:T(8,128)(2,1)} %get-tuple-element.10), channel_id=1, source_target_pairs={{0,8},{8,0},{16,24},{24,16},{1,9},{9,1},{17,25},{25,17},{2,10},{10... | collective-permute-start | bytes 147464 | tf_op jit(solution)/shard_map/ppermute | solution.py:167
  18.9 1.5 %collective-permute-start.1 = (bf16[6,16,256]{2,1,0:T(8,128)(2,1)}, bf16[6,16,256]{2,1,0:T(8,128)(2,1)S(1)}, u32[]{:S(2)}, u32[]{:S(2)}) collective-permute-start(bf16[6,16,256]{2,1,0:T(8,128)(2,1)} %get-tuple-element.11), channel_id=1, source_target_pairs={{0,16},{8,24},{16,0},{24,8},{1,17},{9,25},{17,1},{25,9},{2,18},{10... | collective-permute-start | bytes 147464 | tf_op jit(solution)/shard_map/ppermute | solution.py:167
  20.4 0.0 collective-permute-start.2
  20.4 0.1 iota_add_fusion
  20.6 0.1 add.147
  20.7 0.5 collective-permute-done
  21.2 2.0 %collective-permute-done.1 = bf16[6,16,256]{2,1,0:T(8,128)(2,1)S(1)} collective-permute-done((bf16[6,16,256]{2,1,0:T(8,128)(2,1)}, bf16[6,16,256]{2,1,0:T(8,128)(2,1)S(1)}, u32[]{:S(2)}, u32[]{:S(2)}) %collective-permute-start.1) | collective-permute-done | bytes 49184 | tf_op jit(solution)/shard_map/ppermute | solution.py:167
  23.2 2.4 %collective-permute-done.2 = bf16[6,16,256]{2,1,0:T(8,128)(2,1)S(1)} collective-permute-done((bf16[6,16,256]{2,1,0:T(8,128)(2,1)}, bf16[6,16,256]{2,1,0:T(8,128)(2,1)S(1)}, u32[]{:S(2)}, u32[]{:S(2)}) %collective-permute-start.2) | collective-permute-done | bytes 49184 | tf_op jit(solution)/shard_map/ppermute | solution.py:167
  25.6 0.8 %pad_maximum_fusion.refs_0_ = bf16[4,6,16,256]{3,2,1,0:T(8,128)(2,1)S(1)} fusion(bf16[1,6,16,256]{3,2,1,0:T(8,128)(2,1)S(1)} %bitcast.16, bf16[1,6,16,256]{3,2,1,0:T(8,128)(2,1)S(1)} %bitcast.15, bf16[1,6,16,256]{3,2,1,0:T(8,128)(2,1)S(1)} %bitcast.14, bf16[1,6,16,256]{3,2,1,0:T(8,128)(2,1)} %bitcast.13), kind=kLoop, calls=%fused_computation | loop fusion | flops 294912 | bytes 393216 | tf_op jit(solution)/shard_map/stack | solution.py:168
  26.4 3.7 %collective-permute-start.5 = (bf16[4,6,16,256]{3,2,1,0:T(8,128)(2,1)S(1)}, bf16[4,6,16,256]{3,2,1,0:T(8,128)(2,1)S(1)}, u32[]{:S(2)}, u32[]{:S(2)}) collective-permute-start(bf16[4,6,16,256]{3,2,1,0:T(8,128)(2,1)S(1)} %pad_maximum_fusion.refs_0_), channel_id=1, source_target_pairs={{0,6},{1,7},{2,4},{3,5},{4,2},{5,3},{6,0},{7,1},{8,14},{9,15},{10,... | collective-permute-start | bytes 589832 | tf_op jit(solution)/shard_map/ppermute | solution.py:179
  30.1 0.0 collective-permute-start.4
  30.1 0.8 %collective-permute-start.3 = (bf16[4,6,16,256]{3,2,1,0:T(8,128)(2,1)S(1)}, bf16[4,6,16,256]{3,2,1,0:T(8,128)(2,1)S(1)}, u32[]{:S(2)}, u32[]{:S(2)}) collective-permute-start(bf16[4,6,16,256]{3,2,1,0:T(8,128)(2,1)S(1)} %pad_maximum_fusion.refs_0_), channel_id=1, source_target_pairs={{0,2},{1,3},{2,0},{3,1},{4,6},{5,7},{6,4},{7,5},{8,10},{9,11},{10,... | collective-permute-start | bytes 589832 | tf_op jit(solution)/shard_map/ppermute | solution.py:179
  30.9 0.1 add.140
  31.1 0.1 dynamic-slice_bitcast_fusion
  31.2 0.7 %copy.11.mine_ref = s32[64,1]{1,0:T(8,128)} copy(s32[64,1]{0,1:T(1,128)S(1)} %dynamic-slice_bitcast_fusion) | data formatting | bytes 512 | tf_op jit(solution)/shard_map/broadcast_in_dim | solution.py:207
  31.9 0.0 collective-permute-start.6
  31.9 4.2 %collective-permute-done.5.refs_3_ = bf16[4,6,16,256]{3,2,1,0:T(8,128)(2,1)S(1)} collective-permute-done((bf16[4,6,16,256]{3,2,1,0:T(8,128)(2,1)S(1)}, bf16[4,6,16,256]{3,2,1,0:T(8,128)(2,1)S(1)}, u32[]{:S(2)}, u32[]{:S(2)}) %collective-permute-start.5) | collective-permute-done | bytes 196640 | tf_op jit(solution)/shard_map/ppermute | solution.py:179
  36.1 9.0 %collective-permute-done.4.refs_2_ = bf16[4,6,16,256]{3,2,1,0:T(8,128)(2,1)S(1)} collective-permute-done((bf16[4,6,16,256]{3,2,1,0:T(8,128)(2,1)S(1)}, bf16[4,6,16,256]{3,2,1,0:T(8,128)(2,1)S(1)}, u32[]{:S(2)}, u32[]{:S(2)}) %collective-permute-start.4) | collective-permute-done | bytes 196640 | tf_op jit(solution)/shard_map/ppermute | solution.py:179
  45.1 0.5 collective-permute-start.7
  45.6 0.6 %fusion.row_ref = s32[1,512]{1,0:T(1,128)} fusion(s32[1,512]{1,0:T(1,128)S(1)} %add.140, s32[]{:T(128)} %axis_index.25, s32[]{:T(128)S(6)} %select_n.97, s32[]{:T(128)S(6)} %select_n.93), kind=kLoop, calls=%fused_computation.32 | loop fusion | flops 33792 | bytes 4108 | tf_op jit(solution)/shard_map/add | solution.py:193
  46.3 0.0 collective-permute-done.6.refs_4_
  46.3 0.0 collective-permute-done.9.refs_7_
  46.3 0.3 collective-permute-done.8.refs_6_
  46.5 0.3 collective-permute-done.7.refs_5_
  46.8 0.1 copy-done.4
  46.9 0.1 copy-done.5
  47.0 0.2 copy-done.6
  47.2 0.7 %copy-done.7 = bf16[4,6,16,256]{3,2,1,0:T(8,128)(2,1)} copy-done((bf16[4,6,16,256]{3,2,1,0:T(8,128)(2,1)}, bf16[4,6,16,256]{3,2,1,0:T(8,128)(2,1)S(1)}, u32[]{:S(2)}) %copy-start.7) | copy-done | bytes 196632
  47.9 4.8 %correlate.1 = bf16[2,6,64,512]{3,2,1,0:T(8,128)(2,1)} custom-call(s32[1,512]{1,0:T(1,128)} %fusion.row_ref, s32[64,1]{1,0:T(8,128)} %copy.11.mine_ref, bf16[4,6,16,256]{3,2,1,0:T(8,128)(2,1)} %copy-done, bf16[4,6,16,256]{3,2,1,0:T(8,128)(2,1)} %copy-done.3, bf16[4,6,16,256]{3,2,1,0:T(8,128)(2,1)} %copy-done.2, bf16[4,6,16,256]{3,2,1,0:T(8,128)(2,1)} %copy-done.1, ...), custom_call_target="tpu_custom_call" | custom-call | tf_op jit(solution)/shard_map/correlate/pallas_call | solution.py:199
  (19 shorter events, 0.1 us)
Async XLA Ops:
  0.0 20.4 %copy-start.8 = (s32[256]{0:T(256)S(1)}, s32[256]{0:T(256)}, u32[]{:S(2)}) copy-start(s32[256]{0:T(256)} %param.10) | copy-start | bytes 3076
  15.9 5.4 %collective-permute-start = (bf16[6,16,256]{2,1,0:T(8,128)(2,1)}, bf16[6,16,256]{2,1,0:T(8,128)(2,1)S(1)}, u32[]{:S(2)}, u32[]{:S(2)}) collective-permute-start(bf16[6,16,256]{2,1,0:T(8,128)(2,1)} %get-tuple-element.10), channel_id=1, source_target_pairs={{0,8},{8,0},{16,24},{24,16},{1,9},{9,1},{17,25},{25,17},{2,10},{10... | collective-permute-start | bytes 147464 | tf_op jit(solution)/shard_map/ppermute | solution.py:167
  18.9 4.3 %collective-permute-start.1 = (bf16[6,16,256]{2,1,0:T(8,128)(2,1)}, bf16[6,16,256]{2,1,0:T(8,128)(2,1)S(1)}, u32[]{:S(2)}, u32[]{:S(2)}) collective-permute-start(bf16[6,16,256]{2,1,0:T(8,128)(2,1)} %get-tuple-element.11), channel_id=1, source_target_pairs={{0,16},{8,24},{16,0},{24,8},{1,17},{9,25},{17,1},{25,9},{2,18},{10... | collective-permute-start | bytes 147464 | tf_op jit(solution)/shard_map/ppermute | solution.py:167
  20.4 5.2 %collective-permute-start.2 = (bf16[6,16,256]{2,1,0:T(8,128)(2,1)}, bf16[6,16,256]{2,1,0:T(8,128)(2,1)S(1)}, u32[]{:S(2)}, u32[]{:S(2)}) collective-permute-start(bf16[6,16,256]{2,1,0:T(8,128)(2,1)} %get-tuple-element.12), channel_id=1, source_target_pairs={{0,24},{8,16},{16,8},{24,0},{1,25},{9,17},{17,9},{25,1},{2,26},{10... | collective-permute-start | bytes 147464 | tf_op jit(solution)/shard_map/ppermute | solution.py:167
  26.4 20.4 %copy-start = (bf16[4,6,16,256]{3,2,1,0:T(8,128)(2,1)}, bf16[4,6,16,256]{3,2,1,0:T(8,128)(2,1)S(1)}, u32[]{:S(2)}) copy-start(bf16[4,6,16,256]{3,2,1,0:T(8,128)(2,1)S(1)} %pad_maximum_fusion.refs_0_) | copy-start | bytes 589828
  26.4 9.6 %collective-permute-start.5 = (bf16[4,6,16,256]{3,2,1,0:T(8,128)(2,1)S(1)}, bf16[4,6,16,256]{3,2,1,0:T(8,128)(2,1)S(1)}, u32[]{:S(2)}, u32[]{:S(2)}) collective-permute-start(bf16[4,6,16,256]{3,2,1,0:T(8,128)(2,1)S(1)} %pad_maximum_fusion.refs_0_), channel_id=1, source_target_pairs={{0,6},{1,7},{2,4},{3,5},{4,2},{5,3},{6,0},{7,1},{8,14},{9,15},{10,... | collective-permute-start | bytes 589832 | tf_op jit(solution)/shard_map/ppermute | solution.py:179
  30.1 15.0 %collective-permute-start.4 = (bf16[4,6,16,256]{3,2,1,0:T(8,128)(2,1)S(1)}, bf16[4,6,16,256]{3,2,1,0:T(8,128)(2,1)S(1)}, u32[]{:S(2)}, u32[]{:S(2)}) collective-permute-start(bf16[4,6,16,256]{3,2,1,0:T(8,128)(2,1)S(1)} %pad_maximum_fusion.refs_0_), channel_id=1, source_target_pairs={{0,4},{1,5},{2,6},{3,7},{4,0},{5,1},{6,2},{7,3},{8,12},{9,13},{10,... | collective-permute-start | bytes 589832 | tf_op jit(solution)/shard_map/ppermute | solution.py:179
  30.1 15.0 %collective-permute-start.3 = (bf16[4,6,16,256]{3,2,1,0:T(8,128)(2,1)S(1)}, bf16[4,6,16,256]{3,2,1,0:T(8,128)(2,1)S(1)}, u32[]{:S(2)}, u32[]{:S(2)}) collective-permute-start(bf16[4,6,16,256]{3,2,1,0:T(8,128)(2,1)S(1)} %pad_maximum_fusion.refs_0_), channel_id=1, source_target_pairs={{0,2},{1,3},{2,0},{3,1},{4,6},{5,7},{6,4},{7,5},{8,10},{9,11},{10,... | collective-permute-start | bytes 589832 | tf_op jit(solution)/shard_map/ppermute | solution.py:179
  31.9 14.4 %collective-permute-start.6 = (bf16[4,6,16,256]{3,2,1,0:T(8,128)(2,1)S(1)}, bf16[4,6,16,256]{3,2,1,0:T(8,128)(2,1)S(1)}, u32[]{:S(2)}, u32[]{:S(2)}) collective-permute-start(bf16[4,6,16,256]{3,2,1,0:T(8,128)(2,1)S(1)} %pad_maximum_fusion.refs_0_), channel_id=1, source_target_pairs={{0,1},{1,0},{2,3},{3,2},{4,5},{5,4},{6,7},{7,6},{8,9},{9,8},{10,11... | collective-permute-start | bytes 589832 | tf_op jit(solution)/shard_map/ppermute | solution.py:182
  36.1 10.7 %copy-start.1 = (bf16[4,6,16,256]{3,2,1,0:T(8,128)(2,1)}, bf16[4,6,16,256]{3,2,1,0:T(8,128)(2,1)S(1)}, u32[]{:S(2)}) copy-start(bf16[4,6,16,256]{3,2,1,0:T(8,128)(2,1)S(1)} %collective-permute-done.5.refs_3_) | copy-start | bytes 589828
  36.1 10.2 %collective-permute-start.9 = (bf16[4,6,16,256]{3,2,1,0:T(8,128)(2,1)S(1)}, bf16[4,6,16,256]{3,2,1,0:T(8,128)(2,1)S(1)}, u32[]{:S(2)}, u32[]{:S(2)}) collective-permute-start(bf16[4,6,16,256]{3,2,1,0:T(8,128)(2,1)S(1)} %collective-permute-done.5.refs_3_), channel_id=1, source_target_pairs={{0,1},{1,0},{2,3},{3,2},{4,5},{5,4},{6,7},{7,6},{8,9},{9,8},{10,11... | collective-permute-start | bytes 589832 | tf_op jit(solution)/shard_map/ppermute | solution.py:182
  45.1 1.7 %copy-start.2 = (bf16[4,6,16,256]{3,2,1,0:T(8,128)(2,1)}, bf16[4,6,16,256]{3,2,1,0:T(8,128)(2,1)S(1)}, u32[]{:S(2)}) copy-start(bf16[4,6,16,256]{3,2,1,0:T(8,128)(2,1)S(1)} %collective-permute-done.4.refs_2_) | copy-start | bytes 589828
  45.1 1.4 %collective-permute-start.8 = (bf16[4,6,16,256]{3,2,1,0:T(8,128)(2,1)S(1)}, bf16[4,6,16,256]{3,2,1,0:T(8,128)(2,1)S(1)}, u32[]{:S(2)}, u32[]{:S(2)}) collective-permute-start(bf16[4,6,16,256]{3,2,1,0:T(8,128)(2,1)S(1)} %collective-permute-done.4.refs_2_), channel_id=1, source_target_pairs={{0,1},{1,0},{2,3},{3,2},{4,5},{5,4},{6,7},{7,6},{8,9},{9,8},{10,11... | collective-permute-start | bytes 589832 | tf_op jit(solution)/shard_map/ppermute | solution.py:182
  45.1 1.7 %copy-start.3 = (bf16[4,6,16,256]{3,2,1,0:T(8,128)(2,1)}, bf16[4,6,16,256]{3,2,1,0:T(8,128)(2,1)S(1)}, u32[]{:S(2)}) copy-start(bf16[4,6,16,256]{3,2,1,0:T(8,128)(2,1)S(1)} %collective-permute-done.3.refs_1_) | copy-start | bytes 589828
  45.1 1.7 %collective-permute-start.7 = (bf16[4,6,16,256]{3,2,1,0:T(8,128)(2,1)S(1)}, bf16[4,6,16,256]{3,2,1,0:T(8,128)(2,1)S(1)}, u32[]{:S(2)}, u32[]{:S(2)}) collective-permute-start(bf16[4,6,16,256]{3,2,1,0:T(8,128)(2,1)S(1)} %collective-permute-done.3.refs_1_), channel_id=1, source_target_pairs={{0,1},{1,0},{2,3},{3,2},{4,5},{5,4},{6,7},{7,6},{8,9},{9,8},{10,11... | collective-permute-start | bytes 589832 | tf_op jit(solution)/shard_map/ppermute | solution.py:182
  46.3 0.7 %copy-start.4 = (bf16[4,6,16,256]{3,2,1,0:T(8,128)(2,1)}, bf16[4,6,16,256]{3,2,1,0:T(8,128)(2,1)S(1)}, u32[]{:S(2)}) copy-start(bf16[4,6,16,256]{3,2,1,0:T(8,128)(2,1)S(1)} %collective-permute-done.6.refs_4_) | copy-start | bytes 589828
  46.3 0.8 %copy-start.5 = (bf16[4,6,16,256]{3,2,1,0:T(8,128)(2,1)}, bf16[4,6,16,256]{3,2,1,0:T(8,128)(2,1)S(1)}, u32[]{:S(2)}) copy-start(bf16[4,6,16,256]{3,2,1,0:T(8,128)(2,1)S(1)} %collective-permute-done.9.refs_7_) | copy-start | bytes 589828
  46.5 0.7 %copy-start.6 = (bf16[4,6,16,256]{3,2,1,0:T(8,128)(2,1)}, bf16[4,6,16,256]{3,2,1,0:T(8,128)(2,1)S(1)}, u32[]{:S(2)}) copy-start(bf16[4,6,16,256]{3,2,1,0:T(8,128)(2,1)S(1)} %collective-permute-done.8.refs_6_) | copy-start | bytes 589828
  47.2 0.7 %copy-start.7 = (bf16[4,6,16,256]{3,2,1,0:T(8,128)(2,1)}, bf16[4,6,16,256]{3,2,1,0:T(8,128)(2,1)S(1)}, u32[]{:S(2)}) copy-start(bf16[4,6,16,256]{3,2,1,0:T(8,128)(2,1)S(1)} %collective-permute-done.7.refs_5_) | copy-start | bytes 589828

commit v2 on v1

--- a/solution.py
+++ b/solution.py
@@ -10,7 +10,9 @@
 from jax.sharding import PartitionSpec as P
 
 GROUP = 33
-DEPTH = 256
+PART = 11
+CHANNELIZE_MIB = 40
+CORRELATE_MIB = 40
 VMEM = pl.BlockSpec(memory_space=pltpu.VMEM)
 SMEM = pl.BlockSpec(memory_space=pltpu.SMEM)
 
@@ -34,63 +36,74 @@
 
 
 def channelize(
-    me_ref, volt_ref, proto_ref, table_ref, gains_ref, flag_ref, *refs, groups, frames, stride
+    volt_ref, proto_ref, table_ref, gains_ref, flag_ref, *refs, groups, frames, stride
 ):
     outs = refs[:groups]
-    buf, sems, weights, sums, stage, spectra = refs[groups:]
+    buf, sems, flags, proto, table, given, weights, sums, stage, gains, spectra = refs[groups:]
     inputs = volt_ref.shape[0]
     taps, length = proto_ref.shape
-    used = gains_ref.shape[0]
+    used = gains_ref.shape[1]
     channels = used // 2
     need = frames + taps - 1
-    steps = -(-need // GROUP)
-
-    def fetch(step):
-        part = pl.ds(step * GROUP * length, min(GROUP, need - step * GROUP) * length)
-        return pltpu.make_async_copy(volt_ref.at[:, part], buf.at[:, part], sems.at[step])
-
-    for step in range(steps):
-        fetch(step).start()
-    table = table_ref[...].astype(jnp.float32)
+    parts = -(-need // PART)
+
+    copies = [
+        pltpu.make_async_copy(source, target, sems.at[parts + k])
+        for k, (source, target) in enumerate(
+            ((proto_ref, proto), (table_ref, table), (gains_ref, given), (flag_ref, flags))
+        )
+    ]
+    for part in range(parts):
+        span = pl.ds(part * PART * length, min(PART, need - part * PART) * length)
+        copies.append(
+            pltpu.make_async_copy(volt_ref.at[:, span], buf.at[:, span], sems.at[part])
+        )
+    for copy in copies:
+        copy.start()
+    for copy in copies[:4]:
+        copy.wait()
+    gains[0:inputs, 0:used] = given[...]
+    gains[...] = gains[...].T
+    cosines = table[...].astype(jnp.float32)
     for tap in range(taps):
         weights[tap * stride : (tap + 1) * stride, :] = (
-            table * proto_ref[tap : tap + 1, :]
+            cosines * proto[tap : tap + 1, :]
         ).astype(jnp.bfloat16)
-    for step in range(steps):
-        fetch(step).wait()
-        count = min(GROUP, need - step * GROUP)
-        total = None
-        for low in range(0, length, DEPTH):
-            rows = [
-                buf[:, (step * GROUP + f) * length + low : (step * GROUP + f) * length + low + DEPTH]
-                for f in range(count)
-            ]
-            part = lax.dot_general(
-                jnp.concatenate(rows, axis=0),
-                weights[:, low : low + DEPTH],
-                (((1,), (1,)), ((), ())),
-                preferred_element_type=jnp.float32,
-            )
-            total = part if total is None else total + part
-        sums[step * GROUP : step * GROUP + count] = total.reshape(count, inputs, taps * stride)
-    for first in range(0, frames, 16):
-        count = min(16, frames - first)
-        raw = None
-        for tap in range(taps):
-            piece = sums[first + tap : first + tap + count, :, tap * stride : tap * stride + used]
-            raw = piece if raw is None else raw + piece
-        stage[first * inputs : (first + count) * inputs, 0:used] = raw.reshape(count * inputs, used)
+    for copy in copies[4:]:
+        copy.wait()
+    done = 0
+    for low in range(0, need, GROUP):
+        count = min(GROUP, need - low)
+        rows = [buf[:, (low + f) * length : (low + f + 1) * length] for f in range(count)]
+        total = lax.dot_general(
+            jnp.concatenate(rows, axis=0),
+            weights[...],
+            (((1,), (1,)), ((), ())),
+            preferred_element_type=jnp.float32,
+        )
+        sums[low : low + count] = total.reshape(count, inputs, taps * stride)
+        ready = low + count - taps + 1
+        while done < ready:
+            size = min(16, ready - done)
+            raw = None
+            for tap in range(taps):
+                piece = sums[done + tap : done + tap + size, :, tap * stride : tap * stride + used]
+                raw = piece if raw is None else raw + piece
+            stage[done * inputs : (done + size) * inputs, 0:used] = raw.reshape(size * inputs, used)
+            done += size
+    gains_real = gains[pl.ds(0, channels, stride=2), :]
+    gains_imag = gains[pl.ds(1, channels, stride=2), :]
     for i in range(inputs):
         raw = stage[pl.ds(i, frames, stride=inputs), :].T[0:used, :]
         real, imag = raw[0:channels], raw[channels:used]
-        gain_real = gains_ref[0:channels, i : i + 1]
-        gain_imag = gains_ref[channels:used, i : i + 1]
-        keep = 1.0 - flag_ref[i // 2].astype(jnp.float32)
+        gain_real, gain_imag = gains_real[:, i : i + 1], gains_imag[:, i : i + 1]
+        keep = 1.0 - flags[i // 2].astype(jnp.float32)
         spectra[:, i, 0:frames] = ((gain_real * real - gain_imag * imag) * keep).astype(jnp.bfloat16)
         spectra[:, i, frames:] = ((gain_real * imag + gain_imag * real) * keep).astype(jnp.bfloat16)
     each = channels // groups
+    me = lax.axis_index("chan")
     for step in range(groups):
-        outs[step][...] = spectra[pl.ds(partner(me_ref[0], step, groups) * each, each)]
+        outs[step][...] = spectra[pl.ds(partner(me, step, groups) * each, each)]
 
 
 def correlate(row_ref, mine_ref, *refs, frames):
@@ -134,31 +147,44 @@
     each = channels // chan_size
     stride = 64 if used <= 64 else -(-used // 128) * 128
     need = frames + taps - 1
-    steps = -(-need // GROUP)
-
-    gains = complex_gains.reshape(inputs, channels, 2).transpose(2, 1, 0).reshape(used, inputs)
+    lanes = -(-used // 128) * 128
+    in_hbm = pl.BlockSpec(memory_space=pltpu.HBM)
+
+    scratch = [
+        ((inputs, need * length), jnp.bfloat16),
+        ((taps, length), jnp.float32),
+        ((stride, length), jnp.bfloat16),
+        ((inputs, used), jnp.float32),
+        ((taps * stride, length), jnp.bfloat16),
+        ((need, inputs, taps * stride), jnp.float32),
+        ((frames * inputs, lanes), jnp.float32),
+        ((lanes, lanes), jnp.float32),
+        ((channels, inputs, 2 * frames), jnp.bfloat16),
+    ]
+    scratch = [pltpu.VMEM(shape, dtype) for shape, dtype in scratch]
+    scratch[1:1] = [
+        pltpu.SemaphoreType.DMA((-(-need // PART) + 4,)),
+        pltpu.SMEM(flagged.shape, jnp.int32),
+    ]
     spectra = pl.pallas_call(
         functools.partial(channelize, groups=chan_size, frames=frames, stride=stride),
         out_shape=[jax.ShapeDtypeStruct((each, inputs, 2 * frames), jnp.bfloat16)] * chan_size,
-        in_specs=[SMEM, pl.BlockSpec(memory_space=pl.ANY), VMEM, VMEM, VMEM, SMEM],
+        in_specs=[in_hbm] * 5,
         out_specs=[VMEM] * chan_size,
-        scratch_shapes=[
-            pltpu.VMEM((inputs, need * length), jnp.bfloat16),
-            pltpu.SemaphoreType.DMA((steps,)),
-            pltpu.VMEM((taps * stride, length), jnp.bfloat16),
-            pltpu.VMEM((need, inputs, taps * stride), jnp.float32),
-            pltpu.VMEM((frames * inputs, -(-used // 128) * 128), jnp.float32),
-            pltpu.VMEM((channels, inputs, 2 * frames), jnp.bfloat16),
-        ],
-        compiler_params=pltpu.CompilerParams(vmem_limit_bytes=56 * 1024 * 1024),
+        scratch_shapes=scratch,
+        compiler_params=pltpu.CompilerParams(vmem_limit_bytes=CHANNELIZE_MIB * 1024 * 1024),
         name="channelize",
     )(
-        chan_me[None].astype(jnp.int32),
-        voltages,
-        prototype,
-        table_rows(length, channels, stride),
-        gains,
-        flagged,
+        *(
+            pltpu.with_memory_space_constraint(operand, pltpu.HBM)
+            for operand in (
+                voltages,
+                prototype,
+                table_rows(length, channels, stride),
+                complex_gains,
+                flagged,
+            )
+        )
     )
 
     turned = [spectra[0]]
@@ -202,7 +228,7 @@
         in_specs=[VMEM] * (2 + len(pieces)),
         out_specs=VMEM,
         scratch_shapes=[pltpu.VMEM((inputs_all, inputs_all), jnp.bfloat16)],
-        compiler_params=pltpu.CompilerParams(vmem_limit_bytes=56 * 1024 * 1024),
+        compiler_params=pltpu.CompilerParams(vmem_limit_bytes=CORRELATE_MIB * 1024 * 1024),
         name="correlate",
     )(row[None, :], mine[:, None], *pieces)
 

time: 52.9 us -> 45.3 us (0.86)
  Pallas kernels: 19.2 us -> 15.2 us
  local copies, waits for them, and re-layouts: 3.51 us -> 0.45 us
  other arithmetic: 1.59 us -> 0.22 us
  waiting for transfers between devices: 18.7 us -> 19.6 us
    pallas_call x1, Pallas kernels: 14.4 us -> 11.9 us  [local(): pl.pallas_call(functools.partial(channelize, groups=chan_size, frames=fra...]
    unnamed x19 -> x2, local copies, waits for them, and re-layouts: 1.85 us -> 0.01 us
    pallas_call x1, Pallas kernels: 4.76 us -> 3.29 us  [local(): pl.pallas_call(functools.partial(correlate, frames=frames), out_shape=jax...]
    another operation x1, other arithmetic: 0.82 us -> 0.03 us  [local(): turned = jnp.stack(turned)]
    transpose x1 -> x0, local copies, waits for them, and re-layouts: 0.61 us -> none  [local(): complex_gains.reshape(inputs, channels, 2).transpose(2, 1, 0)]
    broadcast_in_dim x2, local copies, waits for them, and re-layouts: 0.77 us -> 0.18 us  [local(): mine[:, None]]
    ppermute x4, waiting for transfers between devices: 0.55 us -> 1.13 us  [local(): pieces += [lax.ppermute(piece, 'panel', swap) for piece in pieces]]
    add x2, other arithmetic: 0.67 us -> 0.09 us  [local(): piece * (chan_size * inputs)]
  transfers between devices with their start and end apart: 10 -> 10, of which waited for: 7 -> 7; matrix products, arithmetic and copies ran while one was open for 3% -> 1% of each run, Pallas kernels for 0% -> 0%
where the time goes in v2:
time: 45.3 us; the launch traced here: 45.2 us
  waiting for transfers between devices  19.6 us (43%)
  Pallas kernels  15.2 us (34%)
  starting transfers between devices  9.57 us (21%)
    ppermute x3, waiting for transfers between devices, local(): pieces.append(lax.ppermute(turned, 'panel', pairs))  13.8 us
    pallas_call x1, Pallas kernels, local(): pl.pallas_call(functools.partial(channelize, groups=chan_size, frames=fra...  11.9 us
    ppermute x3, waiting for transfers between devices, local(): turned.append(lax.ppermute(spectra[step], 'chan', pairs))  4.69 us
    ppermute x3, starting transfers between devices, local(): turned.append(lax.ppermute(spectra[step], 'chan', pairs))  4.57 us
    ppermute x3, starting transfers between devices, local(): pieces.append(lax.ppermute(turned, 'panel', pairs))  4.45 us
    pallas_call x1, Pallas kernels, local(): pl.pallas_call(functools.partial(correlate, frames=frames), out_shape=jax...  3.29 us
    ppermute x4, waiting for transfers between devices, local(): pieces += [lax.ppermute(piece, 'panel', swap) for piece in pieces]  1.13 us
  transfers between devices with their start and end apart: 10, of which 7 were waited for; matrix products, arithmetic and copies ran while one was open for 1% of the time, Pallas kernels for 0%

profile of v2, /device:TPU:0, one launch (start us, length us, event | category | flops | bytes accessed | tf_op | source)
XLA Modules:
  0.0 45.2 jit_solution(839126212599222982)
XLA Ops:
  0.0 0.0 copy-start
  0.0 11.9 %channelize.1 = (bf16[6,16,256]{2,1,0:T(8,128)(2,1)S(1)}, bf16[6,16,256]{2,1,0:T(8,128)(2,1)S(1)}, bf16[6,16,256]{2,1,0:T(8,128)(2,1)S(1)}, bf16[6,16,256]{2,1,0:T(8,128)(2,1)S(1)}) custom-call(bf16[16,536576]{1,0:T(8,128)(2,1)} %volt_ref.1, f32[4,4096]{1,0:T(4,128)} %proto_ref.1, bf16[64,4096]{1,0:T(8,128)(2,1)} %constant.106.clone.table_ref, ...), custom_call_target="tpu_custom_call" | custom-call | tf_op jit(solution)/shard_map/channelize/pallas_call | solution.py:169
  11.9 3.0 %collective-permute-start = (bf16[6,16,256]{2,1,0:T(8,128)(2,1)S(1)}, bf16[6,16,256]{2,1,0:T(8,128)(2,1)S(1)}, u32[]{:S(2)}, u32[]{:S(2)}) collective-permute-start(bf16[6,16,256]{2,1,0:T(8,128)(2,1)S(1)} %get-tuple-element.10), channel_id=1, source_target_pairs={{0,8},{8,0},{16,24},{24,16},{1,9},{9,1},{17,25},{25,17},{2,10},{10... | collective-permute-start | bytes 147464 | tf_op jit(solution)/shard_map/ppermute | solution.py:193
  15.0 1.5 %collective-permute-start.1 = (bf16[6,16,256]{2,1,0:T(8,128)(2,1)S(1)}, bf16[6,16,256]{2,1,0:T(8,128)(2,1)S(1)}, u32[]{:S(2)}, u32[]{:S(2)}) collective-permute-start(bf16[6,16,256]{2,1,0:T(8,128)(2,1)S(1)} %get-tuple-element.11), channel_id=1, source_target_pairs={{0,16},{8,24},{16,0},{24,8},{1,17},{9,25},{17,1},{25,9},{2,18},{10... | collective-permute-start | bytes 147464 | tf_op jit(solution)/shard_map/ppermute | solution.py:193
  16.5 0.0 collective-permute-start.2
  16.5 0.0 copy-done
  16.5 0.1 iota_add_fusion
  16.6 0.1 add.147
  16.8 0.2 collective-permute-done
  17.0 2.0 %collective-permute-done.1 = bf16[6,16,256]{2,1,0:T(8,128)(2,1)S(1)} collective-permute-done((bf16[6,16,256]{2,1,0:T(8,128)(2,1)S(1)}, bf16[6,16,256]{2,1,0:T(8,128)(2,1)S(1)}, u32[]{:S(2)}, u32[]{:S(2)}) %collective-permute-start.1) | collective-permute-done | bytes 49184 | tf_op jit(solution)/shard_map/ppermute | solution.py:193
  19.1 2.4 %collective-permute-done.2 = bf16[6,16,256]{2,1,0:T(8,128)(2,1)S(1)} collective-permute-done((bf16[6,16,256]{2,1,0:T(8,128)(2,1)S(1)}, bf16[6,16,256]{2,1,0:T(8,128)(2,1)S(1)}, u32[]{:S(2)}, u32[]{:S(2)}) %collective-permute-start.2) | collective-permute-done | bytes 49184 | tf_op jit(solution)/shard_map/ppermute | solution.py:193
  21.5 3.7 %collective-permute-start.5 = (bf16[4,6,16,256]{3,2,1,0:T(8,128)(2,1)S(1)}, bf16[4,6,16,256]{3,2,1,0:T(8,128)(2,1)S(1)}, u32[]{:S(2)}, u32[]{:S(2)}) collective-permute-start(bf16[4,6,16,256]{3,2,1,0:T(8,128)(2,1)S(1)} %pad_maximum_fusion.refs_0_), channel_id=1, source_target_pairs={{0,6},{1,7},{2,4},{3,5},{4,2},{5,3},{6,0},{7,1},{8,14},{9,15},{10,... | collective-permute-start | bytes 589832 | tf_op jit(solution)/shard_map/ppermute | solution.py:205
  25.2 0.0 collective-permute-start.4
  25.2 0.8 %collective-permute-start.3 = (bf16[4,6,16,256]{3,2,1,0:T(8,128)(2,1)S(1)}, bf16[4,6,16,256]{3,2,1,0:T(8,128)(2,1)S(1)}, u32[]{:S(2)}, u32[]{:S(2)}) collective-permute-start(bf16[4,6,16,256]{3,2,1,0:T(8,128)(2,1)S(1)} %pad_maximum_fusion.refs_0_), channel_id=1, source_target_pairs={{0,2},{1,3},{2,0},{3,1},{4,6},{5,7},{6,4},{7,5},{8,10},{9,11},{10,... | collective-permute-start | bytes 589832 | tf_op jit(solution)/shard_map/ppermute | solution.py:205
  26.0 0.1 add.140
  26.1 0.1 dynamic-slice_bitcast_fusion
  26.2 0.1 copy.8.mine_ref
  26.3 0.0 collective-permute-start.6
  26.3 4.8 %collective-permute-done.5.refs_3_ = bf16[4,6,16,256]{3,2,1,0:T(8,128)(2,1)S(1)} collective-permute-done((bf16[4,6,16,256]{3,2,1,0:T(8,128)(2,1)S(1)}, bf16[4,6,16,256]{3,2,1,0:T(8,128)(2,1)S(1)}, u32[]{:S(2)}, u32[]{:S(2)}) %collective-permute-start.5) | collective-permute-done | bytes 196640 | tf_op jit(solution)/shard_map/ppermute | solution.py:205
  31.1 0.0 collective-permute-start.9
  31.1 9.0 %collective-permute-done.4.refs_2_ = bf16[4,6,16,256]{3,2,1,0:T(8,128)(2,1)S(1)} collective-permute-done((bf16[4,6,16,256]{3,2,1,0:T(8,128)(2,1)S(1)}, bf16[4,6,16,256]{3,2,1,0:T(8,128)(2,1)S(1)}, u32[]{:S(2)}, u32[]{:S(2)}) %collective-permute-start.4) | collective-permute-done | bytes 196640 | tf_op jit(solution)/shard_map/ppermute | solution.py:205
  40.2 0.0 collective-permute-start.8
  40.2 0.0 collective-permute-done.3.refs_1_
  40.2 0.5 %collective-permute-start.7 = (bf16[4,6,16,256]{3,2,1,0:T(8,128)(2,1)S(1)}, bf16[4,6,16,256]{3,2,1,0:T(8,128)(2,1)S(1)}, u32[]{:S(2)}, u32[]{:S(2)}) collective-permute-start(bf16[4,6,16,256]{3,2,1,0:T(8,128)(2,1)S(1)} %collective-permute-done.3.refs_1_), channel_id=1, source_target_pairs={{0,1},{1,0},{2,3},{3,2},{4,5},{5,4},{6,7},{7,6},{8,9},{9,8},{10,11... | collective-permute-start | bytes 589832 | tf_op jit(solution)/shard_map/ppermute | solution.py:208
  40.7 0.1 fusion.row_ref
  40.7 0.0 collective-permute-done.6.refs_4_
  40.7 0.0 collective-permute-done.9.refs_7_
  40.8 0.8 %collective-permute-done.8.refs_6_ = bf16[4,6,16,256]{3,2,1,0:T(8,128)(2,1)S(1)} collective-permute-done((bf16[4,6,16,256]{3,2,1,0:T(8,128)(2,1)S(1)}, bf16[4,6,16,256]{3,2,1,0:T(8,128)(2,1)S(1)}, u32[]{:S(2)}, u32[]{:S(2)}) %collective-permute-start.8) | collective-permute-done | bytes 196640 | tf_op jit(solution)/shard_map/ppermute | solution.py:208
  41.6 0.3 collective-permute-done.7.refs_5_
  41.9 3.3 %correlate.1 = bf16[2,6,64,512]{3,2,1,0:T(8,128)(2,1)} custom-call(s32[1,512]{1,0:T(1,128)S(1)} %fusion.row_ref, s32[64,1]{1,0:T(8,128)S(1)} %copy.8.mine_ref, bf16[4,6,16,256]{3,2,1,0:T(8,128)(2,1)S(1)} %pad_maximum_fusion.refs_0_, bf16[4,6,16,256]{3,2,1,0:T(8,128)(2,1)S(1)} %collective-permute-done.3.refs_1_, ...), custom_call_target="tpu_custom_call" | custom-call | tf_op jit(solution)/shard_map/correlate/pallas_call | solution.py:225
  (3 shorter events, 0.1 us)
Async XLA Ops:
  0.0 16.5 %copy-start = (s32[256]{0:T(256)S(1)}, s32[256]{0:T(256)}, u32[]{:S(2)}) copy-start(s32[256]{0:T(256)} %param.10) | copy-start | bytes 3076
  11.9 5.1 %collective-permute-start = (bf16[6,16,256]{2,1,0:T(8,128)(2,1)S(1)}, bf16[6,16,256]{2,1,0:T(8,128)(2,1)S(1)}, u32[]{:S(2)}, u32[]{:S(2)}) collective-permute-start(bf16[6,16,256]{2,1,0:T(8,128)(2,1)S(1)} %get-tuple-element.10), channel_id=1, source_target_pairs={{0,8},{8,0},{16,24},{24,16},{1,9},{9,1},{17,25},{25,17},{2,10},{10... | collective-permute-start | bytes 147464 | tf_op jit(solution)/shard_map/ppermute | solution.py:193
  15.0 4.1 %collective-permute-start.1 = (bf16[6,16,256]{2,1,0:T(8,128)(2,1)S(1)}, bf16[6,16,256]{2,1,0:T(8,128)(2,1)S(1)}, u32[]{:S(2)}, u32[]{:S(2)}) collective-permute-start(bf16[6,16,256]{2,1,0:T(8,128)(2,1)S(1)} %get-tuple-element.11), channel_id=1, source_target_pairs={{0,16},{8,24},{16,0},{24,8},{1,17},{9,25},{17,1},{25,9},{2,18},{10... | collective-permute-start | bytes 147464 | tf_op jit(solution)/shard_map/ppermute | solution.py:193
  16.5 5.0 %collective-permute-start.2 = (bf16[6,16,256]{2,1,0:T(8,128)(2,1)S(1)}, bf16[6,16,256]{2,1,0:T(8,128)(2,1)S(1)}, u32[]{:S(2)}, u32[]{:S(2)}) collective-permute-start(bf16[6,16,256]{2,1,0:T(8,128)(2,1)S(1)} %get-tuple-element.12), channel_id=1, source_target_pairs={{0,24},{8,16},{16,8},{24,0},{1,25},{9,17},{17,9},{25,1},{2,26},{10... | collective-permute-start | bytes 147464 | tf_op jit(solution)/shard_map/ppermute | solution.py:193
  21.5 9.6 %collective-permute-start.5 = (bf16[4,6,16,256]{3,2,1,0:T(8,128)(2,1)S(1)}, bf16[4,6,16,256]{3,2,1,0:T(8,128)(2,1)S(1)}, u32[]{:S(2)}, u32[]{:S(2)}) collective-permute-start(bf16[4,6,16,256]{3,2,1,0:T(8,128)(2,1)S(1)} %pad_maximum_fusion.refs_0_), channel_id=1, source_target_pairs={{0,6},{1,7},{2,4},{3,5},{4,2},{5,3},{6,0},{7,1},{8,14},{9,15},{10,... | collective-permute-start | bytes 589832 | tf_op jit(solution)/shard_map/ppermute | solution.py:205
  25.2 15.0 %collective-permute-start.4 = (bf16[4,6,16,256]{3,2,1,0:T(8,128)(2,1)S(1)}, bf16[4,6,16,256]{3,2,1,0:T(8,128)(2,1)S(1)}, u32[]{:S(2)}, u32[]{:S(2)}) collective-permute-start(bf16[4,6,16,256]{3,2,1,0:T(8,128)(2,1)S(1)} %pad_maximum_fusion.refs_0_), channel_id=1, source_target_pairs={{0,4},{1,5},{2,6},{3,7},{4,0},{5,1},{6,2},{7,3},{8,12},{9,13},{10,... | collective-permute-start | bytes 589832 | tf_op jit(solution)/shard_map/ppermute | solution.py:205
  25.2 15.0 %collective-permute-start.3 = (bf16[4,6,16,256]{3,2,1,0:T(8,128)(2,1)S(1)}, bf16[4,6,16,256]{3,2,1,0:T(8,128)(2,1)S(1)}, u32[]{:S(2)}, u32[]{:S(2)}) collective-permute-start(bf16[4,6,16,256]{3,2,1,0:T(8,128)(2,1)S(1)} %pad_maximum_fusion.refs_0_), channel_id=1, source_target_pairs={{0,2},{1,3},{2,0},{3,1},{4,6},{5,7},{6,4},{7,5},{8,10},{9,11},{10,... | collective-permute-start | bytes 589832 | tf_op jit(solution)/shard_map/ppermute | solution.py:205
  26.3 14.4 %collective-permute-start.6 = (bf16[4,6,16,256]{3,2,1,0:T(8,128)(2,1)S(1)}, bf16[4,6,16,256]{3,2,1,0:T(8,128)(2,1)S(1)}, u32[]{:S(2)}, u32[]{:S(2)}) collective-permute-start(bf16[4,6,16,256]{3,2,1,0:T(8,128)(2,1)S(1)} %pad_maximum_fusion.refs_0_), channel_id=1, source_target_pairs={{0,1},{1,0},{2,3},{3,2},{4,5},{5,4},{6,7},{7,6},{8,9},{9,8},{10,11... | collective-permute-start | bytes 589832 | tf_op jit(solution)/shard_map/ppermute | solution.py:208
  31.1 9.6 %collective-permute-start.9 = (bf16[4,6,16,256]{3,2,1,0:T(8,128)(2,1)S(1)}, bf16[4,6,16,256]{3,2,1,0:T(8,128)(2,1)S(1)}, u32[]{:S(2)}, u32[]{:S(2)}) collective-permute-start(bf16[4,6,16,256]{3,2,1,0:T(8,128)(2,1)S(1)} %collective-permute-done.5.refs_3_), channel_id=1, source_target_pairs={{0,1},{1,0},{2,3},{3,2},{4,5},{5,4},{6,7},{7,6},{8,9},{9,8},{10,11... | collective-permute-start | bytes 589832 | tf_op jit(solution)/shard_map/ppermute | solution.py:208
  40.2 1.4 %collective-permute-start.8 = (bf16[4,6,16,256]{3,2,1,0:T(8,128)(2,1)S(1)}, bf16[4,6,16,256]{3,2,1,0:T(8,128)(2,1)S(1)}, u32[]{:S(2)}, u32[]{:S(2)}) collective-permute-start(bf16[4,6,16,256]{3,2,1,0:T(8,128)(2,1)S(1)} %collective-permute-done.4.refs_2_), channel_id=1, source_target_pairs={{0,1},{1,0},{2,3},{3,2},{4,5},{5,4},{6,7},{7,6},{8,9},{9,8},{10,11... | collective-permute-start | bytes 589832 | tf_op jit(solution)/shard_map/ppermute | solution.py:208
  40.2 1.7 %collective-permute-start.7 = (bf16[4,6,16,256]{3,2,1,0:T(8,128)(2,1)S(1)}, bf16[4,6,16,256]{3,2,1,0:T(8,128)(2,1)S(1)}, u32[]{:S(2)}, u32[]{:S(2)}) collective-permute-start(bf16[4,6,16,256]{3,2,1,0:T(8,128)(2,1)S(1)} %collective-permute-done.3.refs_1_), channel_id=1, source_target_pairs={{0,1},{1,0},{2,3},{3,2},{4,5},{5,4},{6,7},{7,6},{8,9},{9,8},{10,11... | collective-permute-start | bytes 589832 | tf_op jit(solution)/shard_map/ppermute | solution.py:208

commit v3 on v2

--- a/solution.py
+++ b/solution.py
@@ -9,8 +9,9 @@
 from jax.experimental.pallas import tpu as pltpu
 from jax.sharding import PartitionSpec as P
 
-GROUP = 33
-PART = 11
+STEPS = 4
+LEAD = 1
+SMALL = 1024
 CHANNELIZE_MIB = 40
 CORRELATE_MIB = 40
 VMEM = pl.BlockSpec(memory_space=pltpu.VMEM)
@@ -39,13 +40,14 @@
     volt_ref, proto_ref, table_ref, gains_ref, flag_ref, *refs, groups, frames, stride
 ):
     outs = refs[:groups]
-    buf, sems, flags, proto, table, given, weights, sums, stage, gains, spectra = refs[groups:]
+    buf, sems, flags, proto, table, given, weights, sums, stage, gains, tail = refs[groups:]
     inputs = volt_ref.shape[0]
     taps, length = proto_ref.shape
     used = gains_ref.shape[1]
     channels = used // 2
     need = frames + taps - 1
-    parts = -(-need // PART)
+    parts = STEPS
+    group = -(-need // parts)
 
     copies = [
         pltpu.make_async_copy(source, target, sems.at[parts + k])
@@ -54,7 +56,7 @@
         )
     ]
     for part in range(parts):
-        span = pl.ds(part * PART * length, min(PART, need - part * PART) * length)
+        span = pl.ds(part * group * length, min(group, need - part * group) * length)
         copies.append(
             pltpu.make_async_copy(volt_ref.at[:, span], buf.at[:, span], sems.at[part])
         )
@@ -69,57 +71,80 @@
         weights[tap * stride : (tap + 1) * stride, :] = (
             cosines * proto[tap : tap + 1, :]
         ).astype(jnp.bfloat16)
-    for copy in copies[4:]:
+    for copy in copies[4 : 4 + LEAD]:
         copy.wait()
-    done = 0
-    for low in range(0, need, GROUP):
-        count = min(GROUP, need - low)
-        rows = [buf[:, (low + f) * length : (low + f + 1) * length] for f in range(count)]
+
+    def step(index, carry):
+        for part in range(LEAD, parts):
+            pl.when(index == part)(copies[4 + part].wait)
+        low = index * group
+        rows = [
+            buf[:, pl.ds(pl.multiple_of((low + f) * length, length), length)] for f in range(group)
+        ]
         total = lax.dot_general(
             jnp.concatenate(rows, axis=0),
             weights[...],
             (((1,), (1,)), ((), ())),
             preferred_element_type=jnp.float32,
         )
-        sums[low : low + count] = total.reshape(count, inputs, taps * stride)
-        ready = low + count - taps + 1
-        while done < ready:
-            size = min(16, ready - done)
+        sums[pl.ds(low, group)] = total.reshape(group, inputs, taps * stride)
+        first = jnp.maximum(low - taps + 1, 0)
+        for lag in range(0, group, 11):
+            size = min(11, group - lag)
             raw = None
             for tap in range(taps):
-                piece = sums[done + tap : done + tap + size, :, tap * stride : tap * stride + used]
+                piece = sums[
+                    pl.ds(first + lag + tap, size), :, tap * stride : tap * stride + used
+                ]
                 raw = piece if raw is None else raw + piece
-            stage[done * inputs : (done + size) * inputs, 0:used] = raw.reshape(size * inputs, used)
-            done += size
+            target = pl.ds(pl.multiple_of((first + lag) * inputs, inputs), size * inputs)
+            stage[target, 0:used] = raw.reshape(size * inputs, used)
+        return carry
+
+    lax.fori_loop(0, parts, step, 0)
+    lanes = gains.shape[1]
     gains_real = gains[pl.ds(0, channels, stride=2), :]
     gains_imag = gains[pl.ds(1, channels, stride=2), :]
-    for i in range(inputs):
-        raw = stage[pl.ds(i, frames, stride=inputs), :].T[0:used, :]
-        real, imag = raw[0:channels], raw[channels:used]
-        gain_real, gain_imag = gains_real[:, i : i + 1], gains_imag[:, i : i + 1]
-        keep = 1.0 - flags[i // 2].astype(jnp.float32)
-        spectra[:, i, 0:frames] = ((gain_real * real - gain_imag * imag) * keep).astype(jnp.bfloat16)
-        spectra[:, i, frames:] = ((gain_real * imag + gain_imag * real) * keep).astype(jnp.bfloat16)
+
+    def finish(half, carry):
+        base = half * 8
+        shift = lax.rem(lanes - base, lanes)
+        rolled_real = pltpu.roll(gains_real, shift, 1)
+        rolled_imag = pltpu.roll(gains_imag, shift, 1)
+        for k in range(8):
+            raw = stage[pl.ds(base + k, frames, stride=inputs), :].T[0:used, :]
+            real, imag = raw[0:channels], raw[channels:used]
+            gain_real, gain_imag = rolled_real[:, k : k + 1], rolled_imag[:, k : k + 1]
+            keep = 1.0 - flags[half * 4 + k // 2].astype(jnp.float32)
+            tail[half, :, k, 0:frames] = (gain_real * real - gain_imag * imag) * keep
+            tail[half, :, k, frames:] = (gain_real * imag + gain_imag * real) * keep
+        return carry
+
+    lax.fori_loop(0, inputs // 8, finish, 0)
     each = channels // groups
     me = lax.axis_index("chan")
     for step in range(groups):
-        outs[step][...] = spectra[pl.ds(partner(me, step, groups) * each, each)]
+        start = partner(me, step, groups) * each
+        halves = [tail[half, pl.ds(start, each)] for half in range(inputs // 8)]
+        outs[step][...] = jnp.concatenate(halves, axis=1).astype(jnp.bfloat16)
 
 
 def correlate(row_ref, mine_ref, *refs, frames):
-    pieces, out_ref, select = refs[:-2], refs[-2], refs[-1]
-    blocks, each, local = pieces[0].shape[:3]
+    pieces, out_ref, select, products = refs[:-3], refs[-3], refs[-2], refs[-1]
+    each = pieces[0].shape[1]
     inputs = row_ref.shape[1]
     width = mine_ref.shape[0]
+    batch = each if inputs <= SMALL else 1
     select[...] = jnp.where(
         lax.broadcasted_iota(jnp.int32, (inputs, inputs), 0) == row_ref[...], 1.0, 0.0
     ).astype(jnp.bfloat16)
     pick = jnp.where(
         lax.broadcasted_iota(jnp.int32, (width, inputs), 1) == mine_ref[...], 1.0, 0.0
     ).astype(jnp.bfloat16)
-    for j in range(each):
+
+    def channel(j, carry):
         columns = jnp.concatenate(
-            [piece[b, j] for piece in pieces for b in range(blocks)], axis=0
+            [piece[b, j] for piece in pieces for b in range(piece.shape[0])], axis=0
         )
         picked = jnp.dot(pick, columns, preferred_element_type=jnp.float32).astype(jnp.bfloat16)
         swapped = jnp.concatenate([picked[:, frames:], -picked[:, :frames]], axis=1)
@@ -127,11 +152,22 @@
         product = lax.dot_general(
             left, columns, (((1,), (1,)), ((), ())), preferred_element_type=jnp.float32
         )
-        rounded = (product * (1.0 / frames)).astype(jnp.bfloat16)
-        ordered = jnp.dot(rounded, select[...], preferred_element_type=jnp.float32)
-        ordered = ordered.astype(jnp.bfloat16)
-        out_ref[0, j] = ordered[:width]
-        out_ref[1, j] = ordered[width:]
+        rows = pl.ds(pl.multiple_of(j * 2 * width, 2 * width), 2 * width)
+        products[rows, :] = (product * (1.0 / frames)).astype(jnp.bfloat16)
+        return carry
+
+    lax.fori_loop(0, each, channel, 0, unroll=batch)
+
+    def reorder(k, carry):
+        rows = pl.ds(pl.multiple_of(k * batch * 2 * width, 2 * width), batch * 2 * width)
+        ordered = jnp.dot(products[rows, :], select[...], preferred_element_type=jnp.float32)
+        ordered = ordered.astype(jnp.bfloat16).reshape(batch, 2, width, inputs)
+        for i in range(batch):
+            out_ref[0, k * batch + i] = ordered[i, 0]
+            out_ref[1, k * batch + i] = ordered[i, 1]
+        return carry
+
+    lax.fori_loop(0, each // batch, reorder, 0)
 
 
 def local(voltages, prototype, complex_gains, flagged, station_order):
@@ -147,23 +183,24 @@
     each = channels // chan_size
     stride = 64 if used <= 64 else -(-used // 128) * 128
     need = frames + taps - 1
+    padded = -(-need // STEPS) * STEPS
     lanes = -(-used // 128) * 128
     in_hbm = pl.BlockSpec(memory_space=pltpu.HBM)
 
     scratch = [
-        ((inputs, need * length), jnp.bfloat16),
+        ((inputs, padded * length), jnp.bfloat16),
         ((taps, length), jnp.float32),
         ((stride, length), jnp.bfloat16),
         ((inputs, used), jnp.float32),
         ((taps * stride, length), jnp.bfloat16),
-        ((need, inputs, taps * stride), jnp.float32),
-        ((frames * inputs, lanes), jnp.float32),
+        ((padded + taps, inputs, taps * stride), jnp.float32),
+        (((padded + taps) * inputs, lanes), jnp.float32),
         ((lanes, lanes), jnp.float32),
-        ((channels, inputs, 2 * frames), jnp.bfloat16),
+        ((inputs // 8, channels, 8, 2 * frames), jnp.float32),
     ]
     scratch = [pltpu.VMEM(shape, dtype) for shape, dtype in scratch]
     scratch[1:1] = [
-        pltpu.SemaphoreType.DMA((-(-need // PART) + 4,)),
+        pltpu.SemaphoreType.DMA((STEPS + 4,)),
         pltpu.SMEM(flagged.shape, jnp.int32),
     ]
     spectra = pl.pallas_call(
@@ -187,25 +224,30 @@
         )
     )
 
-    turned = [spectra[0]]
+    own = spectra[0][None]
+    rest = []
     for step in range(1, chan_size):
         pairs = [(i, partner(i, step, chan_size)) for i in range(chan_size)]
-        turned.append(lax.ppermute(spectra[step], "chan", pairs))
-    turned = jnp.stack(turned)
+        rest.append(lax.ppermute(spectra[step], "chan", pairs))
+    rest = jnp.stack(rest)
 
     cores = 2 if panel_size % 2 == 0 else 1
     chips = panel_size // cores
-    pieces = [turned]
-    for step in range(1, chips):
+
+    def along(shard, step):
         pairs = [
             (i * cores + k, partner(i, step, chips) * cores + k)
             for i in range(chips)
             for k in range(cores)
         ]
-        pieces.append(lax.ppermute(turned, "panel", pairs))
+        return lax.ppermute(shard, "panel", pairs)
+
+    shards = [(own, rest)]
+    shards += [(along(own, step), along(rest, step)) for step in range(1, chips)]
     if cores == 2:
         swap = [(i, i ^ 1) for i in range(panel_size)]
-        pieces += [lax.ppermute(piece, "panel", swap) for piece in pieces]
+        shards += [tuple(lax.ppermute(part, "panel", swap) for part in shard) for shard in shards]
+    pieces = [part for shard in shards for part in shard]
 
     inputs_all = 2 * station_order.shape[0]
     width = inputs_all // panel_size
@@ -227,7 +269,10 @@
         out_shape=jax.ShapeDtypeStruct((2, each, width, inputs_all), jnp.bfloat16),
         in_specs=[VMEM] * (2 + len(pieces)),
         out_specs=VMEM,
-        scratch_shapes=[pltpu.VMEM((inputs_all, inputs_all), jnp.bfloat16)],
+        scratch_shapes=[
+            pltpu.VMEM((inputs_all, inputs_all), jnp.bfloat16),
+            pltpu.VMEM((each * 2 * width, inputs_all), jnp.bfloat16),
+        ],
         compiler_params=pltpu.CompilerParams(vmem_limit_bytes=CORRELATE_MIB * 1024 * 1024),
         name="correlate",
     )(row[None, :], mine[:, None], *pieces)

time: 45.3 us -> 40.8 us (0.901)
  waiting for transfers between devices: 19.6 us -> 13.3 us
  starting transfers between devices: 9.57 us -> 14.5 us
  Pallas kernels: 15.2 us -> 12.1 us
    ppermute x10 -> x17, waiting for transfers between devices: 19.6 us -> 13.3 us  [the longest x6 7.53 us: along(): return lax.ppermute(shard, 'panel', pairs)]
    ppermute x10 -> x17, starting transfers between devices: 9.57 us -> 14.5 us  [the longest x6 9.12 us: along(): return lax.ppermute(shard, 'panel', pairs)]
    pallas_call x1, Pallas kernels: 11.9 us -> 9.41 us  [local(): pl.pallas_call(functools.partial(channelize, groups=chan_size, frames=fra...]
    pallas_call x1, Pallas kernels: 3.29 us -> 2.72 us  [local(): pl.pallas_call(functools.partial(correlate, frames=frames), out_shape=jax...]
  transfers between devices with their start and end apart: 10 -> 17, of which waited for: 7 -> 7; matrix products, arithmetic and copies ran while one was open for 1% -> 2% of each run, Pallas kernels for 0% -> 0%
where the time goes in v3:
time: 40.8 us; the launch traced here: 40.7 us
  starting transfers between devices  14.5 us (36%)
  waiting for transfers between devices  13.3 us (33%)
  Pallas kernels  12.1 us (30%)
  local copies, waits for them, and re-layouts  0.45 us (1%)
    pallas_call x1, Pallas kernels, local(): pl.pallas_call(functools.partial(channelize, groups=chan_size, frames=fra...  9.41 us
    ppermute x6, starting transfers between devices, along(): return lax.ppermute(shard, 'panel', pairs)  9.12 us
    ppermute x6, waiting for transfers between devices, along(): return lax.ppermute(shard, 'panel', pairs)  7.53 us
    ppermute x3, waiting for transfers between devices, local(): rest.append(lax.ppermute(spectra[step], 'chan', pairs))  4.23 us
    ppermute x3, starting transfers between devices, local(): rest.append(lax.ppermute(spectra[step], 'chan', pairs))  3.49 us
    pallas_call x1, Pallas kernels, local(): pl.pallas_call(functools.partial(correlate, frames=frames), out_shape=jax...  2.72 us
    ppermute x8, starting transfers between devices, local(): lax.ppermute(part, 'panel', swap)  1.87 us
    ppermute x8, waiting for transfers between devices, local(): lax.ppermute(part, 'panel', swap)  1.5 us
  transfers between devices with their start and end apart: 17, of which 7 were waited for; matrix products, arithmetic and copies ran while one was open for 2% of the time, Pallas kernels for 0%

profile of v3, /device:TPU:0, one launch (start us, length us, event | category | flops | bytes accessed | tf_op | source)
XLA Modules:
  0.0 40.7 jit_solution(16195882687805102093)
XLA Ops:
  0.0 9.4 %channelize.1 = (bf16[6,16,256]{2,1,0:T(8,128)(2,1)S(1)}, bf16[6,16,256]{2,1,0:T(8,128)(2,1)S(1)}, bf16[6,16,256]{2,1,0:T(8,128)(2,1)S(1)}, bf16[6,16,256]{2,1,0:T(8,128)(2,1)S(1)}) custom-call(bf16[16,536576]{1,0:T(8,128)(2,1)} %volt_ref.1, f32[4,4096]{1,0:T(4,128)} %proto_ref.1, bf16[64,4096]{1,0:T(8,128)(2,1)} %constant.106.clone.table_ref, ...), custom_call_target="tpu_custom_call" | custom-call | tf_op jit(solution)/shard_map/channelize/pallas_call | solution.py:206
  9.4 0.6 %collective-permute-start.9 = (bf16[1,6,16,256]{3,2,1,0:T(8,128)(2,1)S(1)}, bf16[1,6,16,256]{3,2,1,0:T(8,128)(2,1)S(1)}, u32[]{:S(2)}, u32[]{:S(2)}) collective-permute-start(bf16[1,6,16,256]{3,2,1,0:T(8,128)(2,1)S(1)} %bitcast.6), channel_id=1, source_target_pairs={{0,1},{1,0},{2,3},{3,2},{4,5},{5,4},{6,7},{7,6},{8,9},{9,8},{10,11... | collective-permute-start | bytes 147464 | tf_op jit(solution)/shard_map/ppermute | solution.py:249
  10.0 4.7 %collective-permute-start.7 = (bf16[1,6,16,256]{3,2,1,0:T(8,128)(2,1)S(1)}, bf16[1,6,16,256]{3,2,1,0:T(8,128)(2,1)S(1)}, u32[]{:S(2)}, u32[]{:S(2)}) collective-permute-start(bf16[1,6,16,256]{3,2,1,0:T(8,128)(2,1)S(1)} %bitcast.7), channel_id=1, source_target_pairs={{0,6},{1,7},{2,4},{3,5},{4,2},{5,3},{6,0},{7,1},{8,14},{9,15},{10,... | collective-permute-start | bytes 147464 | tf_op jit(solution)/shard_map/ppermute | solution.py:243
  14.6 1.5 %collective-permute-start = (bf16[6,16,256]{2,1,0:T(8,128)(2,1)S(1)}, bf16[6,16,256]{2,1,0:T(8,128)(2,1)S(1)}, u32[]{:S(2)}, u32[]{:S(2)}) collective-permute-start(bf16[6,16,256]{2,1,0:T(8,128)(2,1)S(1)} %get-tuple-element.10), channel_id=1, source_target_pairs={{0,8},{8,0},{16,24},{24,16},{1,9},{9,1},{17,25},{25,17},{2,10},{10... | collective-permute-start | bytes 147464 | tf_op jit(solution)/shard_map/ppermute | solution.py:231
  16.1 1.5 %collective-permute-start.1 = (bf16[6,16,256]{2,1,0:T(8,128)(2,1)S(1)}, bf16[6,16,256]{2,1,0:T(8,128)(2,1)S(1)}, u32[]{:S(2)}, u32[]{:S(2)}) collective-permute-start(bf16[6,16,256]{2,1,0:T(8,128)(2,1)S(1)} %get-tuple-element.11), channel_id=1, source_target_pairs={{0,16},{8,24},{16,0},{24,8},{1,17},{9,25},{17,1},{25,9},{2,18},{10... | collective-permute-start | bytes 147464 | tf_op jit(solution)/shard_map/ppermute | solution.py:231
  17.7 0.5 %collective-permute-start.2 = (bf16[6,16,256]{2,1,0:T(8,128)(2,1)S(1)}, bf16[6,16,256]{2,1,0:T(8,128)(2,1)S(1)}, u32[]{:S(2)}, u32[]{:S(2)}) collective-permute-start(bf16[6,16,256]{2,1,0:T(8,128)(2,1)S(1)} %get-tuple-element.12), channel_id=1, source_target_pairs={{0,24},{8,16},{16,8},{24,0},{1,25},{9,17},{17,9},{25,1},{2,26},{10... | collective-permute-start | bytes 147464 | tf_op jit(solution)/shard_map/ppermute | solution.py:231
  18.1 0.1 iota_add_fusion
  18.3 0.1 add.140
  18.4 0.3 collective-permute-done
  18.7 1.5 %collective-permute-done.1 = bf16[6,16,256]{2,1,0:T(8,128)(2,1)S(1)} collective-permute-done((bf16[6,16,256]{2,1,0:T(8,128)(2,1)S(1)}, bf16[6,16,256]{2,1,0:T(8,128)(2,1)S(1)}, u32[]{:S(2)}, u32[]{:S(2)}) %collective-permute-start.1) | collective-permute-done | bytes 49184 | tf_op jit(solution)/shard_map/ppermute | solution.py:231
  20.2 2.4 %collective-permute-done.2 = bf16[6,16,256]{2,1,0:T(8,128)(2,1)S(1)} collective-permute-done((bf16[6,16,256]{2,1,0:T(8,128)(2,1)S(1)}, bf16[6,16,256]{2,1,0:T(8,128)(2,1)S(1)}, u32[]{:S(2)}, u32[]{:S(2)}) %collective-permute-start.2) | collective-permute-done | bytes 49184 | tf_op jit(solution)/shard_map/ppermute | solution.py:231
  22.7 0.5 %collective-permute-start.8 = (bf16[3,6,16,256]{3,2,1,0:T(8,128)(2,1)S(1)}, bf16[3,6,16,256]{3,2,1,0:T(8,128)(2,1)S(1)}, u32[]{:S(2)}, u32[]{:S(2)}) collective-permute-start(bf16[3,6,16,256]{3,2,1,0:T(8,128)(2,1)S(1)} %pad_maximum_fusion.refs_1_), channel_id=1, source_target_pairs={{0,6},{1,7},{2,4},{3,5},{4,2},{5,3},{6,0},{7,1},{8,14},{9,15},{10,... | collective-permute-start | bytes 442376 | tf_op jit(solution)/shard_map/ppermute | solution.py:243
  23.2 0.0 collective-permute-done.9.refs_8_
  23.2 0.6 %collective-permute-start.6 = (bf16[3,6,16,256]{3,2,1,0:T(8,128)(2,1)S(1)}, bf16[3,6,16,256]{3,2,1,0:T(8,128)(2,1)S(1)}, u32[]{:S(2)}, u32[]{:S(2)}) collective-permute-start(bf16[3,6,16,256]{3,2,1,0:T(8,128)(2,1)S(1)} %pad_maximum_fusion.refs_1_), channel_id=1, source_target_pairs={{0,4},{1,5},{2,6},{3,7},{4,0},{5,1},{6,2},{7,3},{8,12},{9,13},{10,... | collective-permute-start | bytes 442376 | tf_op jit(solution)/shard_map/ppermute | solution.py:243
  23.8 0.0 collective-permute-done.7.refs_6_
  23.8 3.3 %collective-permute-start.4 = (bf16[3,6,16,256]{3,2,1,0:T(8,128)(2,1)S(1)}, bf16[3,6,16,256]{3,2,1,0:T(8,128)(2,1)S(1)}, u32[]{:S(2)}, u32[]{:S(2)}) collective-permute-start(bf16[3,6,16,256]{3,2,1,0:T(8,128)(2,1)S(1)} %pad_maximum_fusion.refs_1_), channel_id=1, source_target_pairs={{0,2},{1,3},{2,0},{3,1},{4,6},{5,7},{6,4},{7,5},{8,10},{9,11},{10,... | collective-permute-start | bytes 442376 | tf_op jit(solution)/shard_map/ppermute | solution.py:243
  27.1 0.0 collective-permute-done.5.refs_4_
  27.1 0.0 collective-permute-start.15
  27.1 0.1 fusion.row_ref
  27.2 0.1 add.147
  27.4 0.6 %collective-permute-start.10 = (bf16[3,6,16,256]{3,2,1,0:T(8,128)(2,1)S(1)}, bf16[3,6,16,256]{3,2,1,0:T(8,128)(2,1)S(1)}, u32[]{:S(2)}, u32[]{:S(2)}) collective-permute-start(bf16[3,6,16,256]{3,2,1,0:T(8,128)(2,1)S(1)} %pad_maximum_fusion.refs_1_), channel_id=1, source_target_pairs={{0,1},{1,0},{2,3},{3,2},{4,5},{5,4},{6,7},{7,6},{8,9},{9,8},{10,11... | collective-permute-start | bytes 442376 | tf_op jit(solution)/shard_map/ppermute | solution.py:249
  27.9 0.4 %collective-permute-done.15.refs_14_ = bf16[1,6,16,256]{3,2,1,0:T(8,128)(2,1)S(1)} collective-permute-done((bf16[1,6,16,256]{3,2,1,0:T(8,128)(2,1)S(1)}, bf16[1,6,16,256]{3,2,1,0:T(8,128)(2,1)S(1)}, u32[]{:S(2)}, u32[]{:S(2)}) %collective-permute-start.15) | collective-permute-done | bytes 49184 | tf_op jit(solution)/shard_map/ppermute | solution.py:249
  28.4 0.2 collective-permute-start.13
  28.5 2.7 %collective-permute-done.8.refs_7_ = bf16[3,6,16,256]{3,2,1,0:T(8,128)(2,1)S(1)} collective-permute-done((bf16[3,6,16,256]{3,2,1,0:T(8,128)(2,1)S(1)}, bf16[3,6,16,256]{3,2,1,0:T(8,128)(2,1)S(1)}, u32[]{:S(2)}, u32[]{:S(2)}) %collective-permute-start.8) | collective-permute-done | bytes 147488 | tf_op jit(solution)/shard_map/ppermute | solution.py:243
  31.3 0.0 collective-permute-start.16
  31.3 4.8 %collective-permute-done.6.refs_5_ = bf16[3,6,16,256]{3,2,1,0:T(8,128)(2,1)S(1)} collective-permute-done((bf16[3,6,16,256]{3,2,1,0:T(8,128)(2,1)S(1)}, bf16[3,6,16,256]{3,2,1,0:T(8,128)(2,1)S(1)}, u32[]{:S(2)}, u32[]{:S(2)}) %collective-permute-start.6) | collective-permute-done | bytes 147488 | tf_op jit(solution)/shard_map/ppermute | solution.py:243
  36.1 0.5 %collective-permute-start.12 = (bf16[3,6,16,256]{3,2,1,0:T(8,128)(2,1)S(1)}, bf16[3,6,16,256]{3,2,1,0:T(8,128)(2,1)S(1)}, u32[]{:S(2)}, u32[]{:S(2)}) collective-permute-start(bf16[3,6,16,256]{3,2,1,0:T(8,128)(2,1)S(1)} %collective-permute-done.4.refs_3_), channel_id=1, source_target_pairs={{0,1},{1,0},{2,3},{3,2},{4,5},{5,4},{6,7},{7,6},{8,9},{9,8},{10,11... | collective-permute-start | bytes 442376 | tf_op jit(solution)/shard_map/ppermute | solution.py:249
  36.6 0.1 collective-permute-start.11
  36.7 0.1 dynamic-slice_bitcast_fusion
  36.8 0.1 copy.8.mine_ref
  36.9 1.0 %collective-permute-done.11.refs_10_ = bf16[1,6,16,256]{3,2,1,0:T(8,128)(2,1)S(1)} collective-permute-done((bf16[1,6,16,256]{3,2,1,0:T(8,128)(2,1)S(1)}, bf16[1,6,16,256]{3,2,1,0:T(8,128)(2,1)S(1)}, u32[]{:S(2)}, u32[]{:S(2)}) %collective-permute-start.11) | collective-permute-done | bytes 49184 | tf_op jit(solution)/shard_map/ppermute | solution.py:249
  37.9 2.7 %correlate.1 = bf16[2,6,64,512]{3,2,1,0:T(8,128)(2,1)} custom-call(s32[1,512]{1,0:T(1,128)S(1)} %fusion.row_ref, s32[64,1]{1,0:T(8,128)S(1)} %copy.8.mine_ref, bf16[1,6,16,256]{3,2,1,0:T(8,128)(2,1)S(1)} %bitcast.10, bf16[3,6,16,256]{3,2,1,0:T(8,128)(2,1)S(1)} %pad_maximum_fusion.refs_1_, bf16[1,6,16,256]{3,2,1,0:T(8,128)(2,1)S(1)} %collective-permute-done.3.refs_2_, ...), custom_call_target="tpu_custom_call" | custom-call | tf_op jit(solution)/shard_map/correlate/pallas_call | solution.py:267
  (15 shorter events, 0.1 us)
Async XLA Ops:
  0.0 18.1 %copy-start = (s32[256]{0:T(256)S(1)}, s32[256]{0:T(256)}, u32[]{:S(2)}) copy-start(s32[256]{0:T(256)} %param.10) | copy-start | bytes 3076
  9.4 13.8 %collective-permute-start.9 = (bf16[1,6,16,256]{3,2,1,0:T(8,128)(2,1)S(1)}, bf16[1,6,16,256]{3,2,1,0:T(8,128)(2,1)S(1)}, u32[]{:S(2)}, u32[]{:S(2)}) collective-permute-start(bf16[1,6,16,256]{3,2,1,0:T(8,128)(2,1)S(1)} %bitcast.6), channel_id=1, source_target_pairs={{0,1},{1,0},{2,3},{3,2},{4,5},{5,4},{6,7},{7,6},{8,9},{9,8},{10,11... | collective-permute-start | bytes 147464 | tf_op jit(solution)/shard_map/ppermute | solution.py:249
  10.0 13.8 %collective-permute-start.7 = (bf16[1,6,16,256]{3,2,1,0:T(8,128)(2,1)S(1)}, bf16[1,6,16,256]{3,2,1,0:T(8,128)(2,1)S(1)}, u32[]{:S(2)}, u32[]{:S(2)}) collective-permute-start(bf16[1,6,16,256]{3,2,1,0:T(8,128)(2,1)S(1)} %bitcast.7), channel_id=1, source_target_pairs={{0,6},{1,7},{2,4},{3,5},{4,2},{5,3},{6,0},{7,1},{8,14},{9,15},{10,... | collective-permute-start | bytes 147464 | tf_op jit(solution)/shard_map/ppermute | solution.py:243
  14.6 4.1 %collective-permute-start = (bf16[6,16,256]{2,1,0:T(8,128)(2,1)S(1)}, bf16[6,16,256]{2,1,0:T(8,128)(2,1)S(1)}, u32[]{:S(2)}, u32[]{:S(2)}) collective-permute-start(bf16[6,16,256]{2,1,0:T(8,128)(2,1)S(1)} %get-tuple-element.10), channel_id=1, source_target_pairs={{0,8},{8,0},{16,24},{24,16},{1,9},{9,1},{17,25},{25,17},{2,10},{10... | collective-permute-start | bytes 147464 | tf_op jit(solution)/shard_map/ppermute | solution.py:231
  16.1 4.1 %collective-permute-start.1 = (bf16[6,16,256]{2,1,0:T(8,128)(2,1)S(1)}, bf16[6,16,256]{2,1,0:T(8,128)(2,1)S(1)}, u32[]{:S(2)}, u32[]{:S(2)}) collective-permute-start(bf16[6,16,256]{2,1,0:T(8,128)(2,1)S(1)} %get-tuple-element.11), channel_id=1, source_target_pairs={{0,16},{8,24},{16,0},{24,8},{1,17},{9,25},{17,1},{25,9},{2,18},{10... | collective-permute-start | bytes 147464 | tf_op jit(solution)/shard_map/ppermute | solution.py:231
  17.7 5.0 %collective-permute-start.2 = (bf16[6,16,256]{2,1,0:T(8,128)(2,1)S(1)}, bf16[6,16,256]{2,1,0:T(8,128)(2,1)S(1)}, u32[]{:S(2)}, u32[]{:S(2)}) collective-permute-start(bf16[6,16,256]{2,1,0:T(8,128)(2,1)S(1)} %get-tuple-element.12), channel_id=1, source_target_pairs={{0,24},{8,16},{16,8},{24,0},{1,25},{9,17},{17,9},{25,1},{2,26},{10... | collective-permute-start | bytes 147464 | tf_op jit(solution)/shard_map/ppermute | solution.py:231
  18.7 8.4 %collective-permute-start.5 = (bf16[1,6,16,256]{3,2,1,0:T(8,128)(2,1)S(1)}, bf16[1,6,16,256]{3,2,1,0:T(8,128)(2,1)S(1)}, u32[]{:S(2)}, u32[]{:S(2)}) collective-permute-start(bf16[1,6,16,256]{3,2,1,0:T(8,128)(2,1)S(1)} %bitcast.8), channel_id=1, source_target_pairs={{0,4},{1,5},{2,6},{3,7},{4,0},{5,1},{6,2},{7,3},{8,12},{9,13},{10,... | collective-permute-start | bytes 147464 | tf_op jit(solution)/shard_map/ppermute | solution.py:243
  20.2 7.1 %collective-permute-start.3 = (bf16[1,6,16,256]{3,2,1,0:T(8,128)(2,1)S(1)}, bf16[1,6,16,256]{3,2,1,0:T(8,128)(2,1)S(1)}, u32[]{:S(2)}, u32[]{:S(2)}) collective-permute-start(bf16[1,6,16,256]{3,2,1,0:T(8,128)(2,1)S(1)} %bitcast.9), channel_id=1, source_target_pairs={{0,2},{1,3},{2,0},{3,1},{4,6},{5,7},{6,4},{7,5},{8,10},{9,11},{10,... | collective-permute-start | bytes 147464 | tf_op jit(solution)/shard_map/ppermute | solution.py:243
  22.7 8.6 %collective-permute-start.8 = (bf16[3,6,16,256]{3,2,1,0:T(8,128)(2,1)S(1)}, bf16[3,6,16,256]{3,2,1,0:T(8,128)(2,1)S(1)}, u32[]{:S(2)}, u32[]{:S(2)}) collective-permute-start(bf16[3,6,16,256]{3,2,1,0:T(8,128)(2,1)S(1)} %pad_maximum_fusion.refs_1_), channel_id=1, source_target_pairs={{0,6},{1,7},{2,4},{3,5},{4,2},{5,3},{6,0},{7,1},{8,14},{9,15},{10,... | collective-permute-start | bytes 442376 | tf_op jit(solution)/shard_map/ppermute | solution.py:243
  23.2 12.8 %collective-permute-start.6 = (bf16[3,6,16,256]{3,2,1,0:T(8,128)(2,1)S(1)}, bf16[3,6,16,256]{3,2,1,0:T(8,128)(2,1)S(1)}, u32[]{:S(2)}, u32[]{:S(2)}) collective-permute-start(bf16[3,6,16,256]{3,2,1,0:T(8,128)(2,1)S(1)} %pad_maximum_fusion.refs_1_), channel_id=1, source_target_pairs={{0,4},{1,5},{2,6},{3,7},{4,0},{5,1},{6,2},{7,3},{8,12},{9,13},{10,... | collective-permute-start | bytes 442376 | tf_op jit(solution)/shard_map/ppermute | solution.py:243
  23.8 12.2 %collective-permute-start.4 = (bf16[3,6,16,256]{3,2,1,0:T(8,128)(2,1)S(1)}, bf16[3,6,16,256]{3,2,1,0:T(8,128)(2,1)S(1)}, u32[]{:S(2)}, u32[]{:S(2)}) collective-permute-start(bf16[3,6,16,256]{3,2,1,0:T(8,128)(2,1)S(1)} %pad_maximum_fusion.refs_1_), channel_id=1, source_target_pairs={{0,2},{1,3},{2,0},{3,1},{4,6},{5,7},{6,4},{7,5},{8,10},{9,11},{10,... | collective-permute-start | bytes 442376 | tf_op jit(solution)/shard_map/ppermute | solution.py:243
  27.1 1.2 %collective-permute-start.15 = (bf16[1,6,16,256]{3,2,1,0:T(8,128)(2,1)S(1)}, bf16[1,6,16,256]{3,2,1,0:T(8,128)(2,1)S(1)}, u32[]{:S(2)}, u32[]{:S(2)}) collective-permute-start(bf16[1,6,16,256]{3,2,1,0:T(8,128)(2,1)S(1)} %collective-permute-done.7.refs_6_), channel_id=1, source_target_pairs={{0,1},{1,0},{2,3},{3,2},{4,5},{5,4},{6,7},{7,6},{8,9},{9,8},{10,11... | collective-permute-start | bytes 147464 | tf_op jit(solution)/shard_map/ppermute | solution.py:249
  27.4 10.6 %collective-permute-start.10 = (bf16[3,6,16,256]{3,2,1,0:T(8,128)(2,1)S(1)}, bf16[3,6,16,256]{3,2,1,0:T(8,128)(2,1)S(1)}, u32[]{:S(2)}, u32[]{:S(2)}) collective-permute-start(bf16[3,6,16,256]{3,2,1,0:T(8,128)(2,1)S(1)} %pad_maximum_fusion.refs_1_), channel_id=1, source_target_pairs={{0,1},{1,0},{2,3},{3,2},{4,5},{5,4},{6,7},{7,6},{8,9},{9,8},{10,11... | collective-permute-start | bytes 442376 | tf_op jit(solution)/shard_map/ppermute | solution.py:249
  28.4 8.2 %collective-permute-start.13 = (bf16[1,6,16,256]{3,2,1,0:T(8,128)(2,1)S(1)}, bf16[1,6,16,256]{3,2,1,0:T(8,128)(2,1)S(1)}, u32[]{:S(2)}, u32[]{:S(2)}) collective-permute-start(bf16[1,6,16,256]{3,2,1,0:T(8,128)(2,1)S(1)} %collective-permute-done.5.refs_4_), channel_id=1, source_target_pairs={{0,1},{1,0},{2,3},{3,2},{4,5},{5,4},{6,7},{7,6},{8,9},{9,8},{10,11... | collective-permute-start | bytes 147464 | tf_op jit(solution)/shard_map/ppermute | solution.py:249
  31.3 6.7 %collective-permute-start.16 = (bf16[3,6,16,256]{3,2,1,0:T(8,128)(2,1)S(1)}, bf16[3,6,16,256]{3,2,1,0:T(8,128)(2,1)S(1)}, u32[]{:S(2)}, u32[]{:S(2)}) collective-permute-start(bf16[3,6,16,256]{3,2,1,0:T(8,128)(2,1)S(1)} %collective-permute-done.8.refs_7_), channel_id=1, source_target_pairs={{0,1},{1,0},{2,3},{3,2},{4,5},{5,4},{6,7},{7,6},{8,9},{9,8},{10,11... | collective-permute-start | bytes 442376 | tf_op jit(solution)/shard_map/ppermute | solution.py:249
  36.1 1.9 %collective-permute-start.14 = (bf16[3,6,16,256]{3,2,1,0:T(8,128)(2,1)S(1)}, bf16[3,6,16,256]{3,2,1,0:T(8,128)(2,1)S(1)}, u32[]{:S(2)}, u32[]{:S(2)}) collective-permute-start(bf16[3,6,16,256]{3,2,1,0:T(8,128)(2,1)S(1)} %collective-permute-done.6.refs_5_), channel_id=1, source_target_pairs={{0,1},{1,0},{2,3},{3,2},{4,5},{5,4},{6,7},{7,6},{8,9},{9,8},{10,11... | collective-permute-start | bytes 442376 | tf_op jit(solution)/shard_map/ppermute | solution.py:249
  36.1 1.9 %collective-permute-start.12 = (bf16[3,6,16,256]{3,2,1,0:T(8,128)(2,1)S(1)}, bf16[3,6,16,256]{3,2,1,0:T(8,128)(2,1)S(1)}, u32[]{:S(2)}, u32[]{:S(2)}) collective-permute-start(bf16[3,6,16,256]{3,2,1,0:T(8,128)(2,1)S(1)} %collective-permute-done.4.refs_3_), channel_id=1, source_target_pairs={{0,1},{1,0},{2,3},{3,2},{4,5},{5,4},{6,7},{7,6},{8,9},{9,8},{10,11... | collective-permute-start | bytes 442376 | tf_op jit(solution)/shard_map/ppermute | solution.py:249
  36.6 1.3 %collective-permute-start.11 = (bf16[1,6,16,256]{3,2,1,0:T(8,128)(2,1)S(1)}, bf16[1,6,16,256]{3,2,1,0:T(8,128)(2,1)S(1)}, u32[]{:S(2)}, u32[]{:S(2)}) collective-permute-start(bf16[1,6,16,256]{3,2,1,0:T(8,128)(2,1)S(1)} %collective-permute-done.3.refs_2_), channel_id=1, source_target_pairs={{0,1},{1,0},{2,3},{3,2},{4,5},{5,4},{6,7},{7,6},{8,9},{9,8},{10,11... | collective-permute-start | bytes 147464 | tf_op jit(solution)/shard_map/ppermute | solution.py:249
